TPU v7x, 32 devices: a whole 2x2x4 slice. The times are simulated.
32 devices in a mesh: seq: 4 (over x, core), fsdp: 8 (over z, y).
Axes of the slice: x: 2, y: 2, z: 4, core: 2. Of those that a mesh axis runs over, the one named last changes fastest.
Arguments:
- inputs: bfloat16 [16, 2048, 768], P('fsdp', 'seq'), may hold values from -6 to 6
- segment_ids: int32 [16, 1024], P('fsdp'), may hold values from 0 to 15, as said below
- block_ids: int32 [16, 1024], P('fsdp'), may hold values from 0 to 31, as said below
- attn_gain: bfloat16 [768], P('fsdp'), may hold values from 0.099609375 to 1.8984375
- attn_shift: bfloat16 [768], P('fsdp'), may hold values from -3 to 3
- proj_in: bfloat16 [768, 2304], P('fsdp'), may hold values from -0.21875 to 0.21875
- bias_in: bfloat16 [2304], P('fsdp'), may hold values from -2 to 2
- proj_out: bfloat16 [768, 768], P('fsdp'), may hold values from -0.875 to 0.875
- bias_out: bfloat16 [768], P('fsdp'), may hold values from -2 to 2
- mlp_gain: bfloat16 [768], P('fsdp'), may hold values from 0.099609375 to 1.8984375
- mlp_shift: bfloat16 [768], P('fsdp'), may hold values from -3 to 3
- weight_up: bfloat16 [768, 3072], P('fsdp'), may hold values from -0.21875 to 0.21875
- bias_up: bfloat16 [3072], P('fsdp'), may hold values from -3 to 3
- weight_down: bfloat16 [3072, 768], P('fsdp'), may hold values from -0.109375 to 0.109375
- bias_down: bfloat16 [768], P('fsdp'), may hold values from -2 to 2
- cotangent: bfloat16 [16, 2048, 768], P('fsdp', 'seq'), may hold values from -6 to 6
Outputs:
- out_rows: bfloat16 [16, 2048, 768], P('fsdp', 'seq')
- grad_input: float32 [16, 2048, 768], P('fsdp', 'seq')
- grad_attn_gain: float32 [768], P('fsdp')
- grad_attn_shift: float32 [768], P('fsdp')
- grad_proj_in: float32 [768, 2304], P('fsdp')
- grad_bias_in: float32 [2304], P('fsdp')
- grad_proj_out: float32 [768, 768], P('fsdp')
- grad_bias_out: float32 [768], P('fsdp')
- grad_mlp_gain: float32 [768], P('fsdp')
- grad_mlp_shift: float32 [768], P('fsdp')
- grad_weight_up: float32 [768, 3072], P('fsdp')
- grad_bias_up: float32 [3072], P('fsdp')
- grad_weight_down: float32 [3072, 768], P('fsdp')
- grad_bias_down: float32 [768], P('fsdp')
Inputs may be any that keep to these rules, and one draw needn't show every extreme that they name: `segment_ids`: along each sequence the ids start at 0, never fall, and end at 15; equal ids mark one document. One document has exactly 512 tokens and begins between 128 and 384; all others are shorter. `block_ids`: A token's block is the number of whole 16-token blocks between its document's first token and it: 0 at a document's first token, rising by one every 16 tokens of the document.
All inputs are finite; a program needn't handle non-finite values.
Results may differ from a plain program's by a relative error of at most 0.015.
Values may be sent and summed in bfloat16 or wider, within the bound.
A program may use at most 104 MiB of HBM per device.

v0:
```python
import functools
import itertools

import jax
import jax.numpy as jnp
import numpy as np
from jax import lax
from jax.experimental import pallas as pl
from jax.experimental.pallas import tpu as pltpu
from jax.sharding import PartitionSpec as P

HD = 64
QUAD = 4
TILE = 128
HALO = 16
NEAR = TILE + 2 * HALO
EPS = 1e-05
MASKED = -1e30
SEG_STEP = 4096
F32 = jnp.float32
BF16 = jnp.bfloat16
VMEM_BYTES = 62 * 1024 * 1024
MESH = pl.DeviceIdType.MESH
ANY = pl.BlockSpec(memory_space=pl.ANY)
VMEM = pl.BlockSpec(memory_space=pltpu.VMEM)


def dot(a, b):
    return jnp.dot(a, b, preferred_element_type=F32)


def dot_nt(a, b):
    return lax.dot_general(a, b, (((1,), (1,)), ((), ())), preferred_element_type=F32)


def dot_tn(a, b):
    return lax.dot_general(a, b, (((0,), (0,)), ((), ())), preferred_element_type=F32)


def norm_stats(x):
    center = jnp.mean(x, axis=-1, keepdims=True)
    centered = x - center
    inverse = lax.rsqrt(jnp.mean(centered * centered, axis=-1, keepdims=True) + EPS)
    return centered * inverse, inverse


def norm_back(grad, normed, inverse, gain):
    scaled = grad * gain
    first = jnp.mean(scaled, axis=-1, keepdims=True)
    second = jnp.mean(scaled * normed, axis=-1, keepdims=True)
    return inverse * (scaled - first - normed * second)


def partner(u):
    lane = lax.broadcasted_iota(jnp.int32, u.shape, 1)
    half = HD // 2
    return jnp.where(
        lane % HD < half, pltpu.roll(u, u.shape[1] - half, 1), pltpu.roll(u, half, 1)
    )


def whole(shape):
    return pl.BlockSpec(shape, lambda *_: (0,) * len(shape), pipeline_mode=pl.Buffered(1))


def call(kernel, grid, in_specs, out_specs, out_shape, scratch, flops, nbytes, name):
    return pl.pallas_call(
        kernel,
        grid=grid,
        in_specs=in_specs,
        out_specs=out_specs,
        out_shape=out_shape,
        scratch_shapes=scratch,
        compiler_params=pltpu.CompilerParams(vmem_limit_bytes=VMEM_BYTES),
        cost_estimate=pl.CostEstimate(flops=flops, bytes_accessed=nbytes, transcendentals=0),
        name=name,
    )


def like(shape, dtype):
    return jax.ShapeDtypeStruct(shape, dtype)


SMEM = functools.partial(pl.BlockSpec, memory_space=pltpu.SMEM)


def layout(rows, length):
    win = rows - length // 8
    noisy = win + rows + HALO
    used = noisy + rows + 2 * HALO
    return dict(rows=rows, win=win, length=length, noisy=noisy, used=used, keys=-(-used // 256) * 256)


def places(lay, role):
    noisy = role[0] == 0
    second = role[1] == 1
    own_at = jnp.where(noisy, lay["noisy"] + HALO, lay["win"])
    halo_at = jnp.where(
        second,
        lay["noisy"],
        jnp.where(noisy, lay["noisy"] + HALO + lay["rows"], lay["win"] + lay["rows"]),
    )
    return noisy, second, pl.multiple_of(own_at, HALO), pl.multiple_of(halo_at, HALO)


def qkv_rows(lay, where_am, n, x, xb, xc, w, b, gain, shift, cos, sin, q_out, k_out, v_out, a_out):
    width = x.shape[2]
    rows, win = lay["rows"], lay["win"]
    noisy, second, own_at, halo_at = where_am

    def norm(v):
        normed, _ = norm_stats(v.astype(F32))
        return (normed * gain + shift).astype(BF16)

    def zeros(at, count):
        for ref in (k_out, v_out, a_out):
            ref[n, at : at + count, :] = jnp.zeros((count, width), BF16)

    def section(a, parts, table, want_q):
        def put(ref, col, value):
            for begin, count, at in parts:
                ref[n, pl.ds(at, count), col : col + value.shape[1]] = value[begin : begin + count]

        put(a_out, 0, a)
        c = cos[table : table + a.shape[0], :]
        s = sin[table : table + a.shape[0], :]
        first = 0 if want_q else width
        for col in range(first, 3 * width, 256):
            part = dot(a, w[:, col : col + 256]) + b[:, col : col + 256]
            for piece in range(2):
                u = part[:, piece * 128 : piece * 128 + 128]
                at_col = col + piece * 128
                if at_col < 2 * width:
                    u = u * c + partner(u) * s
                if at_col < width:
                    q_out[n, :, at_col : at_col + 128] = (u[:rows] * (HD**-0.5)).astype(BF16)
                elif at_col < 2 * width:
                    put(k_out, at_col - width, u.astype(BF16))
                else:
                    put(v_out, at_col - 2 * width, u.astype(BF16))

    zeros(win + rows, 2 * HALO)
    zeros(lay["used"] - HALO, lay["keys"] - lay["used"] + HALO)
    own = jnp.concatenate([norm(x[n]), norm(xc[n, win:, :])], axis=0)
    section(own, ((0, rows, own_at), (rows, HALO, halo_at)), win, True)

    @pl.when(noisy)
    def _():
        section(norm(xb[n]), ((0, rows, win),), win, False)

    @pl.when(jnp.logical_not(noisy))
    def _():
        zeros(lay["noisy"] + HALO, rows)

    @pl.when(second)
    def _():
        section(norm(xc[n, :win, :]), ((0, win, 0),), 0, False)

    @pl.when(jnp.logical_not(second))
    def _():
        zeros(0, win)


def qkv_columns(lay, n, act, at_parts, table, col, count, w, b, cos, sin, q, k, v):
    width, rows = q.shape[2], lay["rows"]

    def put(ref, at_col, value):
        for begin, size, at in at_parts:
            ref[n, pl.ds(at, size), at_col : at_col + 128] = value[begin : begin + size].astype(BF16)

    c = cos[table : table + act.shape[0], :]
    s = sin[table : table + act.shape[0], :]
    part = dot(act, w[:, col : col + count]) + b[:, col : col + count]
    for at_col in range(col, col + count, 128):
        u = part[:, at_col - col : at_col - col + 128]
        if at_col < 2 * width:
            u = u * c + partner(u) * s
        if at_col < width:
            q[n, :, at_col : at_col + 128] = (u[:rows] * (HD**-0.5)).astype(BF16)
        elif at_col < 2 * width:
            put(k, at_col - width, u)
        else:
            put(v, at_col - 2 * width, u)


def qkv_kernel(lay, role, x, xb, xc, w, vec, cos, sin, *outs):
    width = x.shape[2]
    gain, shift, b = vec[0:1, :width], vec[1:2, :width], vec[2:3, : 3 * width]
    qkv_rows(lay, places(lay, role), 0, x, xb, xc, w, b, gain, shift, cos, sin, *outs)


def windows(lay):
    rows, win, length = lay["rows"], lay["win"], lay["length"]
    longest, earliest, latest = length // 2, length // 8, 3 * length // 8
    found = []
    for at in range(0, rows, TILE):
        begin = win + rows
        for origin in range(0, length, rows):
            pos = origin + at
            low = max(pos - longest, 0)
            if origin > 0:
                low = max(low, earliest)
            if pos >= latest + longest:
                low = max(low, earliest + longest)
            begin = min(begin, low - origin + win)
        found.append((begin // TILE * TILE, win + at + TILE + HALO))
    return found


def tile_loop(lay, body):
    for t, (lo, hi) in enumerate(windows(lay)):
        near = lay["noisy"] + t * TILE
        body(t, slice(t * TILE, t * TILE + TILE), slice(lo, hi), slice(near, near + NEAR), hi - lo)


def make_bias(lay, n, codes, queries, biases):
    (bias,) = biases
    groups = {}
    for t, (lo, hi) in enumerate(windows(lay)):
        groups.setdefault(hi - lo, []).append((t, lo))
    for size, tiles in groups.items():
        (t0, lo0), (t1, lo1), number = tiles[0], tiles[-1], len(tiles)
        apart = max(number - 1, 1)
        assert all(tile == (t0 + k * (t1 - t0) // apart, lo0 + k * (lo1 - lo0) // apart) for k, tile in enumerate(tiles))

        def step(k, carry, size=size, t0=t0, lo0=lo0, dt=(t1 - t0) // apart, dlo=(lo1 - lo0) // apart):
            t = t0 + k * dt
            here = pl.ds(pl.multiple_of(t * TILE, TILE), TILE)
            low, high, same = (queries[n, r : r + 1, here] for r in range(3))
            kc = codes[n, pl.ds(pl.multiple_of(lo0 + k * dlo, HALO), size), :]
            ok = jnp.logical_and(kc >= low, kc <= high)
            bias[t, :size, :] = jnp.where(ok, 0.0, MASKED)
            kn = codes[n, pl.ds(pl.multiple_of(lay["noisy"] + t * TILE, HALO), NEAR), :]
            bias[t, size : size + NEAR, :] = jnp.where(kn == same, 0.0, MASKED)
            return carry

        lax.fori_loop(0, number, step, 0)


def stacked(tile):
    lane = lax.broadcasted_iota(jnp.int32, tile.shape, 1)
    zero = jnp.zeros_like(tile)
    return jnp.concatenate(
        [jnp.where(lane // HD == h, tile, zero) for h in range(QUAD)], axis=0
    )


def own_heads(wide):
    return jnp.concatenate(
        [wide[h * HD : h * HD + HD, h * TILE : h * TILE + TILE] for h in range(QUAD)], axis=0
    )


def keys_of(ref, n, cols, lo, near):
    return jnp.concatenate([ref[n, lo, cols], ref[n, near, cols]], axis=0)


def attend(lay, n, cols, q, k, v, o_out, lse_out, lse_at, biases):
    (bias,) = biases

    def body(t, here, lo, near, size):
        qm = stacked(q[n, here, cols])
        kk = keys_of(k, n, cols, lo, near)
        vv = keys_of(v, n, cols, lo, near)
        s = dot_nt(kk, qm) + jnp.concatenate([bias[t, : size + NEAR, :]] * QUAD, axis=1)
        peak = jnp.max(s, axis=0, keepdims=True)
        p = jnp.exp(s - peak)
        total = jnp.sum(p, axis=0, keepdims=True)
        wide = dot_tn(vv, p.astype(BF16)) * (1.0 / total)
        o_out[n, here, cols] = jnp.transpose(own_heads(wide)).astype(BF16)
        lse_out[lse_at, t : t + 1, :] = peak + jnp.log(total)

    tile_loop(lay, body)


def attend_kernel(lay, codes, queries, q, k, v, o_out, lse_out, *biases):
    @pl.when(pl.program_id(1) == 0)
    def _():
        make_bias(lay, 0, codes, queries, biases)

    attend(lay, 0, slice(None), q, k, v, o_out, lse_out, 0, biases)


def attend_back(
    lay, n, cols, q, k, v, m, cols_m, o, do, lse, lse_at, cos, sin, to, col, dq_out, dk_out, dv_out, dk_acc, dv_acc, biases,
):
    rows, win = lay["rows"], lay["win"]
    qw = QUAD * HD

    def lanes(piece):
        return pl.ds(pl.multiple_of(col + piece * 128, 128), 128)

    dk_acc[...] = jnp.zeros_like(dk_acc)
    dv_acc[...] = jnp.zeros_like(dv_acc)
    (bias,) = biases

    def body(t, here, lo, near, size):
        qm = stacked(q[n, here, cols])
        dom = stacked(do[m, here, cols_m])
        kk = keys_of(k, n, cols, lo, near)
        vv = keys_of(v, n, cols, lo, near)
        both = jnp.transpose(do[m, here, cols_m].astype(F32) * o[m, here, cols_m].astype(F32))
        delta = jnp.concatenate(
            [jnp.sum(both[h * HD : h * HD + HD, :], axis=0, keepdims=True) for h in range(QUAD)],
            axis=1,
        )
        s = dot_nt(kk, qm) + jnp.concatenate([bias[t, : size + NEAR, :]] * QUAD, axis=1)
        p = jnp.exp(s - lse[lse_at, t : t + 1, :])
        dp = dot_nt(vv, dom)
        ds = (p * (dp - delta)).astype(BF16)
        pb = p.astype(BF16)
        dv = dot(pb, dom)
        dk = dot(ds, qm)
        dv_acc[lo, :] += dv[:size]
        dk_acc[lo, :] += dk[:size]
        dv_acc[near, :] += dv[size:]
        dk_acc[near, :] += dk[size:]
        wide = dot_tn(kk, ds)
        dq = jnp.transpose(own_heads(wide)) * (HD**-0.5)
        turn = slice(win + t * TILE, win + t * TILE + TILE)
        c, sn = cos[turn, :], sin[turn, :]
        for piece in range(2):
            u = dq[:, piece * 128 : piece * 128 + 128]
            dq_out[to, here, lanes(piece)] = (u * c - partner(u) * sn).astype(BF16)

    tile_loop(lay, body)
    for piece in range(2):
        dv_out[to, :, lanes(piece)] = dv_acc[:, piece * 128 : piece * 128 + 128].astype(BF16)
    half = (cos[win + rows :, :], sin[win + rows :, :])
    own = (cos[win : win + rows, :], sin[win : win + rows, :])
    tables = (
        (0, (cos[: win + rows, :], sin[: win + rows, :])),
        (win + rows, half),
        (lay["noisy"], half),
        (lay["noisy"] + HALO, own),
        (lay["used"] - HALO, half),
    )
    for at, (c, sn) in tables:
        here = slice(at, at + c.shape[0])
        for piece in range(2):
            u = dk_acc[here, piece * 128 : piece * 128 + 128]
            dk_out[to, here, lanes(piece)] = (u * c - partner(u) * sn).astype(BF16)
    spare = lay["keys"] - lay["used"]
    for piece in range(2):
        dk_out[to, lay["used"] :, lanes(piece)] = jnp.zeros((spare, 128), BF16)


def attend_back_kernel(
    lay, codes, queries, q, k, v, o, do, lse, cos, sin, dq_out, dk_out, dv_out, dk_acc, dv_acc, *biases
):
    @pl.when(pl.program_id(1) == 0)
    def _():
        make_bias(lay, 0, codes, queries, biases)

    attend_back(
        lay, 0, slice(None), q, k, v, 0, slice(None), o, do, lse, 0, cos, sin, 0, 0, dq_out, dk_out, dv_out, dk_acc, dv_acc, biases
    )


def bit_of(index, b):
    return (index // (1 << b)) % 2


def other(index, b):
    return index + (1 << b) * (1 - 2 * bit_of(index, b))


class Net:
    def __init__(self, bits, send, recv, sems):
        self.me, self.f, self.bits = lax.axis_index("seq"), lax.axis_index("fsdp"), bits
        self.core, self.x = self.me % 2, self.me // 2
        self.send, self.recv, self.sems = send, recv, sems
        self.used, self.local_used = 0, 0
        self.started = []

    def partners(self):
        return [{"seq": other(self.me, 0)}, {"seq": other(self.me, 1)}] + [
            {"fsdp": other(self.f, b)} for b in range(self.bits)
        ]

    def barrier(self):
        barrier = pltpu.get_barrier_semaphore()
        for device in self.partners():
            pl.semaphore_signal(barrier, inc=1, device_id=device, device_id_type=MESH)
        pl.semaphore_wait(barrier, 2 + self.bits)

    def copy(self, src, dst, device):
        n = self.used
        self.used += 1
        return pltpu.make_async_remote_copy(
            src_ref=src, dst_ref=dst, send_sem=self.send.at[n], recv_sem=self.recv.at[n],
            device_id=device, device_id_type=MESH,
        )

    def local(self, src, dst):
        n = self.local_used
        self.local_used += 1
        return pltpu.make_async_copy(src, dst, self.sems.at[n])

    def fsdp_index(self, done):
        return tuple(slice(None) if b in done else bit_of(self.f, b) for b in range(self.bits - 1, -1, -1))


FRONT_ORDER = (
    "E s i0 i1",
    "T s R0 i2",
    "i0 i1 i2 i0",
    "u0 s i1 s",
    "u1 i2 o i1",
    "V u0 i0 R1",
    "u1 i1 i2 i0",
    "o d0 P0 L0",
    "L1 W H i2",
    "u0 L2 u1 O0",
    "O1 O2 d1 u0",
    "o d0 A d1",
    "P1 d0 u1 A",
    "A d1 o u0",
    "A u0 d0 u1",
    "A d1 d0 A",
    "o u1",
)
FRONT_BITS = {
    "i0": ((2, 0, 1), False),
    "i1": ((2, 1, 0), False),
    "i2": ((2, 1, 0), False),
    "o": ((2, 1, 0), False),
    "u0": ((2, 1, 0), True),
    "u1": ((2, 0, 1), True),
    "d0": ((2, 1, 0), False),
    "d1": ((0, 2, 1), False),
}


class Gather:
    def __init__(self, net, own, full, tail, tail_x=None, tail_core=None, order=None):
        self.net, self.at = net, 0
        mine = net.fsdp_index(())
        self.own = net.local(own.at[tail], full.at[mine + tail])
        self.stages = []
        done = []
        for b in order if order is not None and len(order) == net.bits else range(net.bits - 1, -1, -1):
            here = full.at[net.fsdp_index(done) + tail]
            src = here if done else own.at[tail]
            self.stages.append(net.copy(src, here, {"fsdp": other(net.f, b)}))
            done.append(b)
        everything = (slice(None),) * net.bits
        for region, b in ((tail_x, 1), (tail_core, 0)):
            if region is not None:
                here = full.at[everything + region]
                self.stages.append(net.copy(here, here, {"seq": other(net.me, b)}))

    def advance(self):
        if self.at > len(self.stages):
            return
        if self.at == 0:
            self.own.start()
        else:
            self.stages[self.at - 1].wait_recv()
        if self.at == 1:
            self.own.wait()
        if self.at < len(self.stages):
            self.stages[self.at].start()
        self.at += 1

    def finish(self):
        for stage in self.stages:
            stage.wait_send()


def front_kernel(
    lay, bits, sizes, x, seg, blk, freqs, w_in_s, w_out_s, w_up_s, w_down_s,
    small0, small1, small2, small3, small4, small5, small6, small7,
    w_in, w_out, w_up, w_down, q_out, k_out, v_out, a_out, o_out, lse_out, vec, cos, sin, codes, queries,
    xb, xc, w_vm, q, k, v, a, o, lse, packs, pack, send, recv, sems, *biases,
):
    rows, win, length = lay["rows"], lay["win"], lay["length"]
    width = x.shape[2]
    hidden = w_up_s.shape[1]
    micro = x.shape[0]
    net = Net(bits, send, recv, sems)
    role = (net.x, net.core)
    noisy, second, own_at, halo_at = places(lay, role)
    first = jnp.logical_not(second)
    clean = jnp.logical_not(noisy)
    net.barrier()

    pair, across = {"seq": other(net.me, 0)}, {"seq": other(net.me, 1)}
    rows_across = [net.copy(x.at[n], xb.at[n], across) for n in range(micro)]
    window = (pl.ds(rows - win, win), slice(None))
    target = (pl.ds(0, win), slice(None))
    rows_pair, rows_pair_b = [], []
    for n in range(micro):
        at = net.used
        rows_pair.append(net.copy(x.at[(n,) + window], xc.at[(n,) + target], pair))
        net.used = at
        rows_pair_b.append(net.copy(xb.at[(n,) + window], xc.at[(n,) + target], pair))
    edge_at = pl.multiple_of((1 - net.core) * (rows - HALO), HALO)
    edge = net.copy(x.at[:, pl.ds(edge_at, HALO), :], xc.at[:, pl.ds(win, HALO), :], pair)

    def columns(begin, size):
        return (slice(None), pl.ds(pl.multiple_of(begin, 128), size))

    pack[...] = jnp.zeros_like(pack)
    smalls = (small0, small1, small2, small3, small4, small5, small6, small7)
    for r, (ref, size) in enumerate(zip(smalls, sizes)):
        pack[r : r + 1, :size] = ref[...].astype(F32).reshape(1, size)
    chunks = {"s": Gather(net, pack, packs, (slice(None), slice(None)))}
    half_in, half_out, half_up = 3 * width // 2, width // 2, hidden // 2
    third = half_in // 3
    for n in range(3):
        region = columns(net.core * half_in + n * third, third)
        chunks["i%d" % n] = Gather(net, w_in_s, w_in, region, None, region, FRONT_BITS["i%d" % n][0])
    region = columns(net.core * half_out, half_out)
    chunks["o"] = Gather(net, w_out_s, w_out, region, None, region, FRONT_BITS["o"][0])
    quarter = half_up // 2
    slab = w_down_s.shape[0]
    for n in range(2):
        order, over_x = FRONT_BITS["u%d" % n]
        region = columns(net.core * half_up + n * quarter, quarter)
        part = columns(net.core * half_up + n * quarter + net.x * (quarter // 2), quarter // 2) if over_x else region
        chunks["u%d" % n] = Gather(net, w_up_s, w_up, part, part if over_x else None, region, order)
        order, over_x = FRONT_BITS["d%d" % n]
        begin = net.core * (slab // 2) + n * (slab // 4)
        region = (pl.ds(pl.multiple_of(begin, HALO), slab // 4), slice(None))
        half_region = (pl.ds(pl.multiple_of(begin + net.x * (slab // 8), HALO), slab // 8), slice(None))
        part = half_region if over_x else region
        chunks["d%d" % n] = Gather(net, w_down_s, w_down, part, part if over_x else None, region, order)

    def rows_start(n):
        @pl.when(clean)
        def _():
            rows_across[n].start()

    count = 1 << bits

    def tables():
        block = 48
        assert (win + rows + HALO) % block == 0

        def table_step(n, carry):
            span = pl.ds(pl.multiple_of(n * block, HALO), block)
            position = lax.broadcasted_iota(jnp.int32, (block, 128), 0) + n * block
            shifted = jnp.where(
                position < win + rows, position - win, position - win - rows + jnp.where(second, -HALO, rows)
            )
            turned = (shifted + jnp.where(second, rows, 0)).astype(F32) * freqs[...]
            lane = lax.broadcasted_iota(jnp.int32, (block, 128), 1)
            cos[span, :] = jnp.cos(turned)
            sine = jnp.sin(turned)
            sin[span, :] = jnp.where(lane % HD < HD // 2, -sine, sine)
            return carry

        lax.fori_loop(0, (win + rows + HALO) // block, table_step, 0)
        code = (seg[...] * SEG_STEP + blk[...]).astype(F32)
        base = (seg[...] * SEG_STEP).astype(F32)
        turned_code = jnp.transpose(jnp.concatenate([code, jnp.zeros((8 - micro, length), F32)], axis=0))
        lay_noisy = lay["noisy"]
        for n in range(micro):
            col = turned_code[:, n : n + 1]
            none = lambda count, value: jnp.full((count, 1), value, F32)
            codes[n, :win, :] = jnp.where(second, col[rows - win : rows], -1.0)
            codes[n, win : win + rows, :] = jnp.where(second, col[rows:], col[:rows])
            after, before = col[rows : rows + HALO], col[rows - HALO : rows]
            codes[n, win + rows : lay_noisy, :] = jnp.where(jnp.logical_and(clean, first), after, -1.0)
            codes[n, lay_noisy : lay_noisy + HALO, :] = jnp.where(jnp.logical_and(noisy, second), before, -2.0)
            codes[n, lay_noisy + HALO : lay_noisy + HALO + rows, :] = jnp.where(
                noisy, jnp.where(second, col[rows:], col[:rows]), -2.0
            )
            codes[n, lay["used"] - HALO : lay["used"], :] = jnp.where(jnp.logical_and(noisy, first), after, -2.0)
            codes[n, lay["used"] :, :] = none(lay["keys"] - lay["used"], -2.0)
            own_code = jnp.where(second, code[n : n + 1, rows:], code[n : n + 1, :rows])
            own_base = jnp.where(second, base[n : n + 1, rows:], base[n : n + 1, :rows])
            high = own_code - jnp.where(noisy, 1.0, 0.0)
            queries[n] = jnp.concatenate([own_base, high, own_code, jnp.zeros((5, rows), F32)], axis=0)

    def vectors():
        kinds = sorted(set(sizes))

        def spread_step(n, totals):
            piece = packs[tuple((n // (1 << b)) % 2 for b in range(bits - 1, -1, -1))]
            added = []
            for size, total in zip(kinds, totals):
                wide = size * count - piece.shape[1]
                padded = jnp.concatenate([piece, jnp.zeros((8, wide), F32)], axis=1) if wide > 0 else piece
                lanes = lax.broadcasted_iota(jnp.int32, padded.shape, 1)
                added.append(total + pltpu.roll(jnp.where(lanes < size, padded, 0.0), n * size, 1))
            return tuple(added)

        zero = tuple(jnp.zeros((8, size * count), F32) for size in kinds)
        spread = dict(zip(kinds, lax.fori_loop(0, count, spread_step, zero)))
        for r, size in enumerate(sizes):
            vec[r : r + 1, : size * count] = spread[size][r : r + 1]
            if size * count < vec.shape[1]:
                vec[r : r + 1, size * count :] = jnp.zeros((1, vec.shape[1] - size * count), F32)

    def pass_on(n):
        @pl.when(noisy)
        def _():
            rows_across[n].wait_recv()

        @pl.when(jnp.logical_and(first, noisy))
        def _():
            rows_pair_b[n].start()

        @pl.when(jnp.logical_and(first, clean))
        def _():
            rows_pair[n].start()

    loads = {}

    def load_weights(j):
        slab_in = w_in_s.shape[0]
        for n in range(count):
            at = tuple((n >> b) & 1 for b in range(bits - 1, -1, -1))
            for block in range(2):
                cols = slice(block * half_in + j * third, block * half_in + (j + 1) * third)
                copy = net.local(w_in.at[at + (slice(None), cols)], w_vm.at[n * slab_in : (n + 1) * slab_in, cols])
                copy.start()
                loads.setdefault(j, []).append(copy)

    def norm(value):
        normed, _ = norm_stats(value.astype(F32))
        return (normed * vec[0:1, :width] + vec[1:2, :width]).astype(BF16)

    def zeros(n, at, size):
        for ref in (k, v, a):
            ref[n, at : at + size, :] = jnp.zeros((size, width), BF16)

    def norms():
        def step(n, carry):
            zeros(n, win + rows, 2 * HALO)
            zeros(n, lay["used"] - HALO, lay["keys"] - lay["used"] + HALO)

            @pl.when(clean)
            def _():
                zeros(n, lay["noisy"] + HALO, rows)

            @pl.when(first)
            def _():
                zeros(n, 0, win)

            a[n, pl.ds(own_at, rows), :] = norm(x[n])
            a[n, pl.ds(halo_at, HALO), :] = norm(xc[n, win:, :])
            return carry

        lax.fori_loop(0, micro, step, 0)

    def own_rows(j):
        for load in loads[j]:
            load.wait()

        def step(n, carry):
            act = jnp.concatenate([a[n, pl.ds(own_at, rows), :], a[n, pl.ds(halo_at, HALO), :]], axis=0)
            for block in range(2):
                qkv_columns(
                    lay, n, act, ((0, rows, own_at), (rows, HALO, halo_at)), win, block * half_in + j * third, third,
                    w_vm, vec[2:3, : 3 * width], cos, sin, q, k, v,
                )
            return carry

        lax.fori_loop(0, micro, step, 0)

    def key_rows(n):
        def section(value, at):
            a[n, at : at + value.shape[0], :] = act = norm(value)
            for col in range(width, 3 * width, 384):
                qkv_columns(
                    lay, n, act, ((0, value.shape[0], at),), at, col, 384, w_vm, vec[2:3, : 3 * width], cos, sin, q, k, v
                )

        @pl.when(noisy)
        def _():
            section(xb[n], win)

        @pl.when(second)
        def _():
            for m in range(micro):

                @pl.when(n == m)
                def _(m=m):
                    rows_pair[m].wait_recv()

            section(xc[n, :win, :], 0)

        for store in stores_of(n):
            store.start()

    first_store = net.local_used
    net.local_used += 4 * micro

    def stores_of(n):
        return [
            pltpu.make_async_copy(here.at[n], there.at[n], sems.at[first_store + 4 * n + m])
            for m, (here, there) in enumerate(((q, q_out), (k, k_out), (v, v_out), (a, a_out)))
        ]

    def serve(token):
        if token in chunks:
            chunks[token].advance()
        elif len(token) == 2:
            {"R": rows_start, "P": pass_on, "L": load_weights, "O": own_rows}[token[0]](int(token[1]))
        else:
            {"E": edge.start, "W": edge.wait_recv, "T": tables, "V": vectors, "H": norms}[token]()

    ahead, *after = [part.split() for part in " ".join(FRONT_ORDER).split("A")]
    for token in ahead:
        serve(token)

    quads = width // (QUAD * HD)
    assert micro * quads == len(after)

    def step(index, carry):
        n, h = index // quads, index % quads

        @pl.when(h == 0)
        def _():
            key_rows(n)
            make_bias(lay, n, codes, queries, biases)

        cols = pl.ds(pl.multiple_of(h * QUAD * HD, QUAD * HD), QUAD * HD)
        def serve_all():
            for at, tokens in enumerate(after):
                if tokens:

                    @pl.when(index == at)
                    def _(tokens=tokens):
                        for token in tokens:
                            serve(token)

        attend(lay, n, cols, q, k, v, o, lse, index, biases)
        serve_all()
        return carry

    lax.fori_loop(0, micro * quads, step, 0)
    last = [net.local(o, o_out), net.local(lse, lse_out)]
    for store in last:
        store.start()
    while any(chunk.at <= len(chunk.stages) for chunk in chunks.values()):
        for chunk in chunks.values():
            chunk.advance()
    for chunk in chunks.values():
        chunk.finish()
    for store in stores_of(0) + stores_of(1) + last:
        store.wait()
    edge.wait_send()

    @pl.when(clean)
    def _():
        for n in range(micro):
            rows_across[n].wait_send()

    @pl.when(first)
    def _():
        for n in range(micro):
            rows_pair[n].wait_send()


def gelu_both(u):
    scale = 0.7978845608028654
    square = u * u
    inner = scale * u * (1.0 + 0.044715 * square)
    th = jnp.tanh(inner)
    plus = 0.5 * (1.0 + th)
    slope = plus + 0.5 * u * (1.0 - th * th) * (scale * (1.0 + 3 * 0.044715 * square))
    return (u * plus).astype(BF16), slope


def mlp_kernel(
    o, x, dy, w_out, vec, w_up, b_up, w_down,
    out_rows, dx2_out, do_out, g_w_out, g_w_up, g_b_up, g_w_down, g_vec,
    mid, a2, a2t, inv, acc_out, acc_da,
):
    step = pl.program_id(0)
    last = pl.num_programs(0) - 1
    width = x.shape[1]
    b_out, gain, shift, b_down = (vec[r : r + 1, :width] for r in (3, 4, 5, 7))

    @pl.when(step == 0)
    def _():
        value = x[...].astype(F32) + dot(o[...], w_out[...]) + b_out
        mid[...] = value
        normed, inverse = norm_stats(value)
        inv[...] = inverse
        a = (normed * gain + shift).astype(BF16)
        a2[...] = a
        a2t[...] = jnp.transpose(a)
        acc_out[...] = jnp.zeros_like(acc_out)
        acc_da[...] = jnp.zeros_like(acc_da)

    g, slope = gelu_both(dot(a2[...], w_up[...]) + b_up[6:7, :])
    acc_out[...] += dot(g, w_down[...])
    du32 = dot_nt(dy[...], w_down[...]) * slope
    du = du32.astype(BF16)
    g_b_up[...] = jnp.broadcast_to(jnp.sum(du.astype(F32), axis=0, keepdims=True), g_b_up.shape)
    acc_da[...] += dot_nt(du, w_up[...])
    g_w_down[...] = dot_tn(g, dy[...]).astype(BF16)
    g_w_up[...] = dot(a2t[...], du).astype(BF16)

    @pl.when(step == last)
    def _():
        dyf = dy[...].astype(F32)
        out_rows[...] = (mid[...] + acc_out[...] + b_down).astype(BF16)
        inverse = inv[...]
        value = mid[...]
        normed = (value - jnp.mean(value, axis=-1, keepdims=True)) * inverse
        da = acc_da[...]
        dx2 = dyf + norm_back(da, normed, inverse, gain)
        dx2_out[...] = dx2
        dp = dx2.astype(BF16)
        do_out[...] = dot_nt(dp, w_out[...]).astype(BF16)
        g_w_out[...] = dot_tn(o[...], dp).astype(BF16)
        g_vec[...] = jnp.concatenate(
            [
                jnp.sum(dyf, axis=0, keepdims=True),
                jnp.sum(da * normed, axis=0, keepdims=True),
                jnp.sum(da, axis=0, keepdims=True),
                jnp.sum(dp.astype(F32), axis=0, keepdims=True),
                jnp.zeros((4, dyf.shape[1]), F32),
            ],
            axis=0,
        )


def qkv_back_kernel(lay, role, a, dq, dk, dv, w, da_own, da_main, da_win, g_w, g_b, g_acc):
    width = dq.shape[2]
    rows, win = lay["rows"], lay["win"]
    noisy, second, own_at, halo_at = places(lay, role)

    @pl.when(pl.program_id(0) == 0)
    def _():
        g_acc[...] = jnp.zeros_like(g_acc)
        g_b[...] = jnp.zeros_like(g_b)

    def column_sums(col, value):
        g_b[0:1, col : col + width] += jnp.sum(value.astype(F32), axis=0, keepdims=True)

    def section(parts, query):
        def take(ref):
            return jnp.concatenate([ref[0, pl.ds(at, count), :] for at, count in parts], axis=0)

        at_t = jnp.transpose(take(a))
        key = take(dk)
        value = take(dv)
        g_acc[:, width : 2 * width] += dot(at_t, key)
        g_acc[:, 2 * width :] += dot(at_t, value)
        column_sums(width, key)
        column_sums(2 * width, value)
        total = dot_nt(key, w[:, width : 2 * width]) + dot_nt(value, w[:, 2 * width :])
        if query is not None:
            g_acc[:, :width] += dot(at_t[:, : query.shape[0]], query)
            column_sums(0, query)
            first = total[: query.shape[0]] + dot_nt(query, w[:, :width])
            return first, total[query.shape[0] :]
        return total

    own, near = section(((own_at, rows), (halo_at, HALO)), dq[0])
    da_own[0] = own
    da_win[0, win:, :] = near.astype(BF16)

    @pl.when(noisy)
    def _():
        da_main[0] = section(((win, rows),), None).astype(BF16)

    @pl.when(second)
    def _():
        da_win[0, :win, :] = section(((0, win),), None).astype(BF16)

    @pl.when(pl.program_id(0) == pl.num_programs(0) - 1)
    def _():
        g_w[...] = g_acc[...].astype(BF16)


def final_kernel(x, da, extra, dx2, gain, grad_in, g_vec):
    value = x[...].astype(F32)
    normed, inverse = norm_stats(value)
    grad = da[...] + extra[...].astype(F32)
    grad_in[...] = dx2[...] + norm_back(grad, normed, inverse, gain[...])

    @pl.when(pl.program_id(0) == 0)
    def _():
        g_vec[...] = jnp.zeros_like(g_vec)

    g_vec[0:1, :] += jnp.sum(grad * normed, axis=0, keepdims=True)
    g_vec[1:2, :] += jnp.sum(grad, axis=0, keepdims=True)


def add_to(ref, at, value):
    ref[at] = (ref[at].astype(F32) + value.astype(F32)).astype(BF16)


def for_all(bits, body):
    if bits == 0:
        body(())
        return

    def step(n, carry):
        body(tuple((n // (1 << b)) % 2 for b in range(bits - 1, -1, -1)))
        return carry

    lax.fori_loop(0, 1 << bits, step, 0)


BACK_ORDER = (
    "S s S s",
    "u0 d0 S s",
    "d0 S s u1",
    "u0 d1 S s",
    "d1 S s d2",
    "d0 u0 u2 E",
    "o u2 d0 u1",
    "e d2 d1 u0",
    "o X e A",
    "A A u2 u0",
    "d2 A d1 P0",
    "u1 A o A",
    "u2 T e d2",
    "P1 G0 i0 o",
    "G1 i1 Y0 i0",
    "e d2 i1 G2",
    "i2 N i0 d0",
    "o d1 i2 i1",
    "Y1 N e N",
    "d2 N l i0",
    "i2 l l",
)
BACK_BITS = {
    "u0": ((0, 1, 2), True),
    "u1": ((1, 2, 0), False),
    "u2": ((0, 1, 2), False),
    "d0": ((0, 1, 2), False),
    "d1": ((0, 2, 1), False),
    "d2": ((0, 1, 2), False),
    "o": ((0, 1, 2), False),
    "i0": ((1, 2, 0), False),
    "i1": ((0, 1, 2), False),
    "i2": ((0, 1, 2), False),
}


class Reduce:
    def __init__(self, net, acc, recvs, out, rows, cols, order, over_x):
        bits, self.net, self.at, self.sent = net.bits, net, 0, False
        pair, across = {"seq": other(net.me, 0)}, {"seq": other(net.me, 1)}
        recvs = list(recvs)
        part = (slice(None), slice(None))
        begin, size = rows
        tail = tail_half = (pl.ds(begin, size), cols)
        self.acc, self.steps = acc, [None]
        if over_x:
            piece = size // 2
            part = (pl.ds(pl.multiple_of(net.x * piece, HALO), piece), slice(None))
            away = (pl.ds(pl.multiple_of((1 - net.x) * piece, HALO), piece), slice(None))
            tail = (pl.ds(pl.multiple_of(begin + net.x * piece, HALO), piece), cols)
            got_x = recvs.pop(0)

            def add_x():
                for_all(bits, lambda at: add_to(acc, at + part, got_x[at]))

            self.steps.append((net.copy(acc.at[(slice(None),) * bits + away], got_x, across), add_x))
        done = []
        for b in order if len(order) == bits else range(bits):
            got = recvs.pop(0)

            def index(mine, rest, b=b, done=tuple(done)):
                rest = iter(rest)
                return tuple(
                    mine if p == b else bit_of(net.f, p) if p in done else next(rest) for p in range(bits - 1, -1, -1)
                )

            left = bits - 1 - len(done)

            def add_bit(got=got, b=b, index=index, left=left):
                for_all(left, lambda at: add_to(acc, index(bit_of(net.f, b), at) + part, got[at]))

            src = acc.at[index(1 - bit_of(net.f, b), (slice(None),) * left) + part]
            self.steps.append((net.copy(src, got, {"fsdp": other(net.f, b)}), add_bit))
            done.append(b)
        own = tuple(bit_of(net.f, n) for n in range(bits - 1, -1, -1))
        if over_x:
            before = self.steps[-1][1]

            def keep():
                before()
                out[tail] = acc[own + part]

            self.steps[-1] = (self.steps[-1][0], keep)
            self.steps.append((net.copy(out.at[tail], out.at[tail], across), lambda: None))
        else:
            got_last = recvs.pop(0)

            def last():
                out[tail] = (acc[own].astype(F32) + got_last[...].astype(F32)).astype(BF16)

            self.steps.append((net.copy(acc.at[own], got_last, across), last))
        self.steps.append((net.copy(out.at[tail_half], out.at[tail_half], pair), lambda: None))

    def feed(self, theirs, get):
        def mine():
            for_all(self.net.bits, lambda at: add_to(self.acc, at, get(at)))

        self.steps[0] = (self.net.copy(theirs, self.acc, {"seq": other(self.net.me, 0)}), mine)

    def open(self):
        return self.at <= len(self.steps)

    def advance(self):
        if not self.open():
            return
        if self.at > 0:
            copy, then = self.steps[self.at - 1]
            copy.wait_recv()
            then()
        if self.at < len(self.steps):
            self.steps[self.at][0].start()
        self.at += 1

    def finish(self):
        while self.open():
            self.advance()
        for copy, _ in self.steps[1 if self.sent else 0 :]:
            copy.wait_send()


class SumAll:
    def __init__(self, net, value, recvs):
        self.value, self.recvs, self.at = value, recvs, 0
        devices = [{"seq": other(net.me, b)} for b in range(2)]
        devices += [{"fsdp": other(net.f, b)} for b in range(net.bits)]
        self.copies = []
        for n, device in enumerate(devices):
            src = value if n == 0 else recvs.at[len(devices) + n - 1]
            self.copies.append(net.copy(src, recvs.at[n], device))

    def open(self):
        return self.at <= len(self.copies)

    def advance(self):
        count = len(self.copies)
        if not self.open():
            return
        if self.at > 0:
            n = self.at - 1
            self.copies[n].wait_recv()
            held = self.value[...] if n == 0 else self.recvs[count + n - 1]
            self.recvs[count + n] = held + self.recvs[n]
        if self.at < count:
            self.copies[self.at].start()
        self.at += 1

    def finish(self):
        while self.open():
            self.advance()
        for copy in self.copies:
            copy.wait_send()
        return self.recvs[2 * len(self.copies) - 1]


def back_kernel(
    lay, bits, codes, queries, lse, cos, sin, vec, x, o,
    dy, q, k, v, a, w_in, w_out, w_up, w_down,
    out_rows, grad_in, f_in_out, f_out_out, f_up_out, f_down_out, sums_out, late_out,
    do, recv_parts, rwin,
    acc_in, acc_out, acc_up, acc_down, r_in, r_out, r_up, r_down, f_in, f_out, f_up, f_down,
    sums, sums_recv, late, late_recv, send, recv, sems, *biases,
):
    rows, win, keys = lay["rows"], lay["win"], lay["keys"]
    micro, width = x.shape[0], x.shape[2]
    total = micro * rows
    hidden = vec.shape[1]
    qw = QUAD * HD
    quads = width // qw
    net = Net(bits, send, recv, sems)
    where_am = noisy, second, own_at, halo_at = places(lay, (net.x, net.core))
    first, clean = jnp.logical_not(second), jnp.logical_not(noisy)
    gain = vec[0:1, :width]
    net.barrier()
    every = list(itertools.product(range(2), repeat=bits))
    count = len(every)
    pair, across = {"seq": other(net.me, 0)}, {"seq": other(net.me, 1)}
    slab_down = f_down.shape[0]
    steps = slab_down // 128
    share = count // 2
    wide = share * 128
    whole_index = (slice(None),) * bits
    here, there = net.core, 1 - net.core

    def columns(begin, size):
        return (slice(None), pl.ds(pl.multiple_of(begin, 128), size))

    @pl.when(noisy)
    def _():
        recv_parts[...] = jnp.zeros_like(recv_parts)

    sums[...] = jnp.zeros_like(sums)

    def feed_forward(dyv, wu, wd, w_ov, mid, a2, a2t, inv, acc_y, acc_da, gv, duv, gd, gu, gu_out, sem_w, sem_m):
        block = total // 4

        def loads(index):
            j, h = index // 2, index % 2
            slot = index % 2
            copies = []
            for n in range(share):
                at = pl.multiple_of((h * share + n) * slab_down + j * 128, 128)
                part = pl.ds(n * 128, 128)
                copies.append(pltpu.make_async_copy(w_up.at[:, pl.ds(at, 128)], wu.at[slot, :, part], sem_w.at[slot, 2 * n]))
                copies.append(pltpu.make_async_copy(w_down.at[pl.ds(at, 128), :], wd.at[slot, part, :], sem_w.at[slot, 2 * n + 1]))
            return copies

        first_loads = [pltpu.make_async_copy(w_out, w_ov, sem_m.at[0]), pltpu.make_async_copy(dy, dyv, sem_m.at[1])]
        for load in first_loads + loads(0):
            load.start()
        flat = lambda ref: ref[...].reshape(total, width)
        b_out, gain2, shift2, b_down = (vec[r : r + 1, :width] for r in (3, 4, 5, 7))
        first_loads[0].wait()
        def part_rows(n):
            per = rows // block
            return n // per, pl.ds(pl.multiple_of((n % per) * block, block), block)

        def open_step(n, carry):
            span = pl.ds(pl.multiple_of(n * block, block), block)
            m, sub = part_rows(n)
            value = x[m, sub, :].astype(F32) + dot(o[m, sub, :], w_ov[...]) + b_out
            mid[span, :] = value
            normed, inverse = norm_stats(value)
            inv[span, :] = inverse
            act = (normed * gain2 + shift2).astype(BF16)
            a2[span, :] = act
            a2t[:, span] = jnp.transpose(act)
            return carry

        lax.fori_loop(0, total // block, open_step, 0)
        acc_y[...] = jnp.zeros_like(acc_y)
        acc_da[...] = jnp.zeros_like(acc_da)
        first_loads[1].wait()

        away = columns(there * (width // 2), width // 2)
        near = columns(here * (width // 2), width // 2)
        for j in range(steps):
            chunks["u%d" % j].feed(gu.at[j, there], lambda at, j=j: gu[(j, here) + at])
            chunks["d%d" % j].feed(gd.at[(j,) + whole_index + away], lambda at, j=j: gd[(j,) + at + near])

        def serve_all(index, part):
            for at, tokens in enumerate(in_feed):
                if tokens[part]:

                    @pl.when(index == at)
                    def _(tokens=tokens[part]):
                        for token in tokens:
                            chunks[token].advance()

        def step(index, carry):
            j, h = index // 2, index % 2
            slot = index % 2

            @pl.when(index + 1 < 2 * steps)
            def _():
                for load in loads(index + 1):
                    load.start()

            for load in loads(index):
                load.wait()
            at = [pl.ds(pl.multiple_of((h * share + n) * slab_down + j * 128, 128), 128) for n in range(share)]
            bias = jnp.concatenate([vec[6:7, here_at] for here_at in at], axis=1)
            w_u, w_d = wu[slot], wd[slot]

            def rows_step(r, row):
                for sub in range(2):
                    span = pl.ds(pl.multiple_of((2 * r + sub) * block, block), block)
                    g, slope = gelu_both(dot(a2[span, :], w_u) + bias)
                    gv[span, :] = g
                    acc_y[span, :] += dot(g, w_d)
                    du = (dot_nt(dyv[span, :], w_d) * slope).astype(BF16)
                    duv[span, :] = du
                    row += jnp.sum(du.astype(F32), axis=0, keepdims=True)
                    acc_da[span, :] += dot_nt(du, w_u)
                return row

            row = lax.fori_loop(0, total // (2 * block), rows_step, jnp.zeros((1, wide), F32))
            for n in range(share):
                sums[6:7, at[n]] = row[:, n * 128 : n * 128 + 128]
            serve_all(index, 0)
            slab = width // count

            def half_step(m, carry):
                part = pl.ds(pl.multiple_of(m * (wide // 2), 128), wide // 2)
                g_d = dot_tn(gv[:, part], dyv[...]).astype(BF16)
                for n, low in enumerate(itertools.product(range(2), repeat=bits - 2)):
                    gd[(j, h, m) + low] = g_d[n * 128 : n * 128 + 128]
                g_u = dot(a2t[pl.ds(pl.multiple_of(m * (width // 2), 128), width // 2), :], duv[...]).astype(BF16)
                for n, low in enumerate(itertools.product(range(2), repeat=bits - 1)):
                    gu[(j, h, m) + low] = g_u[n * slab : n * slab + slab]
                return carry

            lax.fori_loop(0, 2, half_step, 0)
            serve_all(index, 1)
            return carry

        lax.fori_loop(0, 2 * steps, step, 0)
        def close_step(n, carry):
            span = pl.ds(pl.multiple_of(n * block, block), block)
            m, sub = part_rows(n)
            dyf = dyv[span, :].astype(F32)
            value = mid[span, :]
            a2[span, :] = (value + acc_y[span, :] + b_down).astype(BF16)
            normed = (value - jnp.mean(value, axis=-1, keepdims=True)) * inv[span, :]
            da = acc_da[span, :]
            dx2 = dyf + norm_back(da, normed, inv[span, :], gain2)
            acc_da[span, :] = dx2
            dp = dx2.astype(BF16)
            dyv[span, :] = dp
            do[m, sub, :] = dot_nt(dp, w_ov[...]).astype(BF16)
            for r, part in ((7, dyf), (4, da * normed), (5, da), (3, dp.astype(F32))):
                sums[r : r + 1, :width] += jnp.sum(part, axis=0, keepdims=True)
            return carry

        lax.fori_loop(0, total // block, close_step, 0)
        puts = []
        for n in range(micro):
            part = pl.ds(n * rows, rows)
            puts.append(pltpu.make_async_copy(acc_da.at[part, :], grad_in.at[n], sem_m.at[2 + 2 * n]))
            puts.append(pltpu.make_async_copy(a2.at[part, :], out_rows.at[n], sem_m.at[3 + 2 * n]))
        for put in puts:
            put.start()
        g_o = dot_tn(flat(o), dyv[...]).astype(BF16)
        slab = width // count
        for n, idx in enumerate(every):
            for c in range(2):
                gu_out[(c,) + idx] = g_o[n * slab : n * slab + slab, c * (width // 2) : (c + 1) * (width // 2)]
        chunks["o"].feed(gu_out.at[there], lambda at: gu_out[(here,) + at])
        for token in after_feed:
            chunks[token].advance()
        for name, chunk in chunks.items():
            if name[0] in "udo":
                assert chunk.at >= 2
                chunk.steps[0][0].wait_send()
                chunk.sent = True
        for put in puts:
            put.wait()

    half_out = width // 2
    slab = width // count
    chunks = {}
    for j in range(steps):
        chunks["u%d" % j] = Reduce(net, acc_up[j], r_up[j], f_up.at[j], (0, slab),
                                   columns(here * wide, wide)[1], *BACK_BITS["u%d" % j])
        chunks["d%d" % j] = Reduce(net, acc_down[j], r_down[j], f_down, (j * 128, 128),
                                   columns(here * half_out, half_out)[1], *BACK_BITS["d%d" % j])
    chunks["o"] = Reduce(net, acc_out, r_out, f_out, (0, slab), columns(here * half_out, half_out)[1], *BACK_BITS["o"])
    chunks["e"] = SumAll(net, sums, sums_recv)
    chunks["l"] = SumAll(net, late, late_recv)
    edge_at = pl.multiple_of((1 - net.core) * (rows - HALO), HALO)
    tokens = " ".join(BACK_ORDER).split()
    feed_end, free, turn = tokens.index("E"), tokens.index("X"), tokens.index("T")
    halves = lambda text, outer, inner: [[half.split() for half in part.split(inner)] for part in text.split(outer)]
    (_,), *in_feed = halves(" ".join(tokens[:feed_end]), "S", "s")
    after_feed = tokens[feed_end + 1 : free]
    early_tokens, *in_attention = [part.split() for part in " ".join(tokens[free + 1 : turn]).split("A")]
    after_attention = tokens[turn + 1 :]
    assert len(in_feed) == 2 * steps and len(in_attention) == micro * quads

    pl.run_scoped(
        feed_forward,
        pltpu.VMEM((total, width), BF16), pltpu.VMEM((2, width, wide), BF16), pltpu.VMEM((2, wide, width), BF16),
        pltpu.VMEM((width, width), BF16), pltpu.VMEM((total, width), F32), pltpu.VMEM((total, width), BF16),
        pltpu.VMEM((width, total), BF16), pltpu.VMEM((total, 1), F32), pltpu.VMEM((total, width), F32),
        pltpu.VMEM((total, width), F32), pltpu.VMEM((total, wide), BF16), pltpu.VMEM((total, wide), BF16),
        pltpu.VMEM((steps,) + (2,) * bits + (128, width), BF16),
        pltpu.VMEM((steps, 2) + (2,) * bits + (width // count, wide), BF16),
        pltpu.VMEM((2,) + (2,) * bits + (width // count, half_out), BF16),
        pltpu.SemaphoreType.DMA((2, 2 * share)), pltpu.SemaphoreType.DMA((2 + 2 * micro,)),
    )

    def backward(dq, dk, dv, w_vm, gin, parts, dwin, sem_l):
        load_w = pltpu.make_async_copy(w_in, w_vm, sem_l.at[0])
        load_w.start()
        p1 = [net.copy(dwin.at[n], rwin.at[n], pair) for n in range(micro)]
        p2 = [net.copy(parts.at[n], recv_parts.at[n], across) for n in range(micro)]
        third = 3 * width // 6
        slab_in = width // count
        for j in range(3):
            chunks["i%d" % j] = Reduce(net, acc_in[j], r_in[j], f_in, (0, slab_in),
                                       columns(here * 3 * third + j * third, third)[1], *BACK_BITS["i%d" % j])
            chunks["i%d" % j].feed(gin.at[j, there], lambda at, j=j: gin[(j, here) + at])

        def pass_on(n):
            p1[n].wait_recv()

            @pl.when(noisy)
            def _():
                @pl.when(first)
                def _():
                    add_to(parts, (n, slice(rows - win, rows), slice(None)), rwin[n, :win, :])

                p2[n].start()

        def attention(qb, kb, vb, dk_acc, dv_acc, load_sems):
            blocks = ((q, qb), (k, kb), (v, vb))

            def loads(index):
                n, h = index // quads, index % quads
                cols = pl.ds(pl.multiple_of(h * qw, qw), qw)
                slot = index % 2
                return [
                    pltpu.make_async_copy(src.at[n, :, cols], dst.at[slot], load_sems.at[slot, m])
                    for m, (src, dst) in enumerate(blocks)
                ]

            for load in loads(0):
                load.start()
            load_w.wait()

            def partial(n):
                key = jnp.concatenate([dk[n, :win, :], dk[n, pl.ds(halo_at, HALO), :]], axis=0)
                value = jnp.concatenate([dv[n, :win, :], dv[n, pl.ds(halo_at, HALO), :]], axis=0)
                w_key, w_value = w_vm[:, width : 2 * width], w_vm[:, 2 * width :]
                dwin[n] = (dot_nt(key, w_key) + dot_nt(value, w_value)).astype(BF16)
                for m in range(micro):

                    @pl.when(n == m)
                    def _(m=m):
                        p1[m].start()

                @pl.when(noisy)
                def _():
                    main = slice(win, win + rows)
                    parts[n] = (dot_nt(dk[n, main, :], w_key) + dot_nt(dv[n, main, :], w_value)).astype(BF16)

            def serve(token):
                if token[0] == "P":
                    pass_on(int(token[1]))
                else:
                    chunks[token].advance()

            for token in early_tokens:
                serve(token)

            def serve_all(index):
                for at, tokens in enumerate(in_attention):
                    if tokens:

                        @pl.when(index == at)
                        def _(tokens=tokens):
                            for token in tokens:
                                serve(token)

            def step(index, carry):
                n, h = index // quads, index % quads
                slot = index % 2

                @pl.when(index + 1 < micro * quads)
                def _():
                    for load in loads(index + 1):
                        load.start()

                @pl.when(h == 0)
                def _():
                    make_bias(lay, n, codes, queries, biases)

                for load in loads(index):
                    load.wait()
                cols = pl.ds(pl.multiple_of(h * qw, qw), qw)
                attend_back(
                    lay, slot, slice(None), qb, kb, vb, n, cols, o, do, lse, index, cos, sin,
                    n, h * qw, dq, dk, dv, dk_acc, dv_acc, biases,
                )
                @pl.when(h == quads - 1)
                def _():
                    partial(n)

                serve_all(index)
                return carry

            lax.fori_loop(0, micro * quads, step, 0)

        pl.run_scoped(
            attention,
            pltpu.VMEM((2, rows, qw), BF16), pltpu.VMEM((2, keys, qw), BF16), pltpu.VMEM((2, keys, qw), BF16),
            pltpu.VMEM((keys, qw), F32), pltpu.VMEM((keys, qw), F32),
            pltpu.SemaphoreType.DMA((2, 3)),
        )

        def projection(av, at_all, at_own, dxv, sem_a, sem_x):
            load_x = pltpu.make_async_copy(grad_in, dxv, sem_x.at[0])
            pltpu.make_async_copy(a.at[0], av, sem_a.at[0]).start()
            load_x.start()
            def turn_step(n, carry):
                pltpu.make_async_copy(a.at[n], av, sem_a.at[n]).wait()
                at_all[n] = jnp.transpose(av[...])
                at_own[n] = jnp.transpose(av[pl.ds(own_at, rows), :])

                @pl.when(n + 1 < micro)
                def _():
                    pltpu.make_async_copy(a.at[n + 1], av, sem_a.at[n + 1]).start()

                return carry

            lax.fori_loop(0, micro, turn_step, 0)
            late[...] = jnp.zeros_like(late)
            def gradient(j):
                for block in range(2):
                    col = block * 3 * third + j * third
                    source, lhs = ((dq, at_own), (dk, at_all), (dv, at_all))[col // width]
                    inside = slice(col % width, col % width + third)
                    part = width // 2

                    def rows_step(m, carry):
                        grad = jnp.zeros((part, third), F32)
                        for n in range(micro):
                            grad += dot(lhs[n, pl.ds(pl.multiple_of(m * part, 128), part), :], source[n, :, inside])
                        for low, at in enumerate(itertools.product(range(2), repeat=bits - 1)):
                            gin[(j, block, m) + at] = grad[low * slab_in : low * slab_in + slab_in].astype(BF16)
                        return carry

                    lax.fori_loop(0, 2, rows_step, 0)
                    ones = jnp.zeros((8, third), F32)
                    for n in range(micro):
                        rhs = source[n, :, inside]
                        ones += dot(jnp.ones((8, rhs.shape[0]), BF16), rhs)
                    row = 2 + col // width
                    late[row : row + 1, inside] = ones[0:1]

            def settle(n):
                @pl.when(clean)
                def _():
                    p2[n].wait_recv()

                    @pl.when(first)
                    def _():
                        add_to(recv_parts, (n, slice(rows - win, rows), slice(None)), rwin[n, :win, :])

                add_to(recv_parts, (n, pl.ds(edge_at, HALO), slice(None)), rwin[n, win:, :])

            def store(m):
                span = pl.ds(pl.multiple_of((m % 2) * (rows // 2), TILE), rows // 2)
                return pltpu.make_async_copy(dxv.at[m // 2, span, :], grad_in.at[m // 2, span, :], sem_x.at[1 + m])

            def norm_part(m):
                n, part = m // 2, m % 2
                size = rows // 2
                span = pl.ds(pl.multiple_of(part * size, TILE), size)
                mine_rows = pl.ds(pl.multiple_of(own_at + part * size, HALO), size)
                da = dot_nt(dq[n, span, :], w_vm[:, :width])
                da += dot_nt(dk[n, mine_rows, :], w_vm[:, width : 2 * width])
                da += dot_nt(dv[n, mine_rows, :], w_vm[:, 2 * width :])
                da += recv_parts[n, span, :].astype(F32)
                normed, inverse = norm_stats(x[n, span, :].astype(F32))
                dxv[n, span, :] += norm_back(da, normed, inverse, gain)
                late[0:1, :] += jnp.sum(da * normed, axis=0, keepdims=True)
                late[1:2, :] += jnp.sum(da, axis=0, keepdims=True)
                store(m).start()

            def serve(token):
                if token in chunks:
                    chunks[token].advance()
                else:
                    {"P": pass_on, "Y": settle, "G": gradient}[token[0]](int(token[1]))

            groups = [part.split() for part in " ".join(after_attention).split("N")]
            assert len(groups) == 1 + 2 * micro
            for token in groups[0]:
                serve(token)
            load_x.wait()

            def norm_step(m, carry):
                norm_part(m)
                for at, tokens in enumerate(groups[1:-1]):
                    if tokens:

                        @pl.when(m == at)
                        def _(tokens=tokens):
                            for token in tokens:
                                serve(token)

                return carry

            lax.fori_loop(0, 2 * micro, norm_step, 0)
            for token in groups[-1]:
                serve(token)
            while any(chunk.open() for chunk in chunks.values()):
                for chunk in chunks.values():
                    chunk.advance()
            sums_out[...] = chunks["e"].finish()
            late_out[...] = chunks["l"].finish()
            for name, chunk in chunks.items():
                if name not in "el":
                    chunk.finish()
            puts = [net.local(src, dst) for src, dst in ((f_in, f_in_out), (f_out, f_out_out), (f_down, f_down_out))]
            for j in range(steps):
                for n in range(count):
                    puts.append(net.local(
                        f_up.at[j, :, pl.ds(n * 128, 128)], f_up_out.at[:, pl.ds(n * slab_down + j * 128, 128)]
                    ))
            for put in puts:
                put.start()
            for put in puts:
                put.wait()
            for m in range(2 * micro):
                store(m).wait()
            for copy in p1:
                copy.wait_send()

            @pl.when(noisy)
            def _():
                for copy in p2:
                    copy.wait_send()

        pl.run_scoped(
            projection,
            pltpu.VMEM((keys, width), BF16), pltpu.VMEM((micro, width, keys), BF16),
            pltpu.VMEM((micro, width, rows), BF16), pltpu.VMEM((micro, rows, width), F32),
            pltpu.SemaphoreType.DMA((micro,)), pltpu.SemaphoreType.DMA((1 + 2 * micro,)),
        )

    third = 3 * width // 6
    pl.run_scoped(
        backward,
        pltpu.VMEM((micro, rows, width), BF16), pltpu.VMEM((micro, keys, width), BF16),
        pltpu.VMEM((micro, keys, width), BF16), pltpu.VMEM((width, 3 * width), BF16),
        pltpu.VMEM((3, 2) + (2,) * bits + (width // count, third), BF16),
        pltpu.VMEM((micro, rows, width), BF16), pltpu.VMEM((micro, win + HALO, width), BF16),
        pltpu.SemaphoreType.DMA((1,)),
    )


def finish_kernel(sizes, sums, late, g_in, g_out, g_up, g_down, o_in, o_out, o_up, o_down, *vectors):
    for src, dst in ((g_in, o_in), (g_out, o_out), (g_up, o_up), (g_down, o_down)):
        dst[...] = src[...].astype(F32)
    f = lax.axis_index("fsdp")
    width = late.shape[1]
    for r, (size, out) in enumerate(zip(sizes, vectors)):
        if r < 2:
            row = late[r : r + 1, :]
        elif r == 2:
            row = jnp.concatenate([late[m : m + 1, :] for m in range(2, 5)], axis=1)
        else:
            row = sums[r : r + 1, :] if sums.shape[1] == size * (width // sizes[0]) else sums[r : r + 1, :width]
        whole_size = row.shape[1]
        row = jnp.broadcast_to(row, (8, whole_size))
        turned = pltpu.roll(row, lax.rem(whole_size - f * size, whole_size), 1)
        out[...] = turned[0, :size]


def front_remote(
    lay, role, sizes, inputs, segment_ids, block_ids, small, weights, freqs, lse_shape, bias_scratch, spans, attn_flops
):
    micro, rows, width = inputs.shape
    keys, win = lay["keys"], lay["win"]
    bits = lax.axis_size("fsdp").bit_length() - 1
    lanes = -(-max(sizes) // 128) * 128
    full = [like((2,) * bits + p.shape, BF16) for p in weights]
    longest = max(sizes) << bits
    table_rows = win + rows + HALO
    shapes = full + [
        like((micro, rows, width), BF16), like((micro, keys, width), BF16), like((micro, keys, width), BF16),
        like((micro, keys, width), BF16), like((micro, rows, width), BF16), like(lse_shape, F32),
        like((8, longest), F32), like((table_rows, 128), F32), like((table_rows, 128), F32),
        like((micro, keys, 1), F32), like((micro, 8, rows), F32),
    ]
    remote = 3 * micro + 1 + (bits + 2) * 9
    outs = pl.pallas_call(
        functools.partial(front_kernel, lay, bits, sizes),
        in_specs=[VMEM] * 16,
        out_specs=[ANY] * 10 + [VMEM] * 5,
        out_shape=shapes,
        scratch_shapes=[
            pltpu.VMEM((micro, rows, width), BF16), pltpu.VMEM((micro, win + HALO, width), BF16),
            pltpu.VMEM((width, 3 * width), BF16), pltpu.VMEM((micro, rows, width), BF16),
            pltpu.VMEM((micro, keys, width), BF16), pltpu.VMEM((micro, keys, width), BF16),
            pltpu.VMEM((micro, keys, width), BF16), pltpu.VMEM((micro, rows, width), BF16),
            pltpu.VMEM(lse_shape, F32), pltpu.VMEM((2,) * bits + (8, lanes), F32), pltpu.VMEM((8, lanes), F32),
            pltpu.SemaphoreType.DMA((remote,)), pltpu.SemaphoreType.DMA((remote,)),
            pltpu.SemaphoreType.DMA((96,)),
        ] + bias_scratch,
        compiler_params=pltpu.CompilerParams(
            vmem_limit_bytes=VMEM_BYTES, collective_id=0, has_side_effects=True
        ),
        cost_estimate=pl.CostEstimate(flops=2 * attn_flops, bytes_accessed=40 << 20, transcendentals=0),
        name="front",
    )(inputs, segment_ids, block_ids, freqs, *weights, *small)
    joined = [w.reshape((-1, w.shape[-1])) for w in outs[:4]]
    return tuple(joined) + tuple(outs[4:])


def front_native(
    lay, role, sizes, inputs, segment_ids, block_ids, small, weights, freqs, lse_shape, bias_scratch, spans, attn_flops
):
    micro, rows, width = inputs.shape
    keys, win, length = lay["keys"], lay["win"], lay["length"]
    clean, half = role[0], role[1]
    pairs = [(0, 1), (1, 0), (2, 3), (3, 2)]
    xb = lax.ppermute(inputs, "seq", [(2, 0), (3, 1)])
    xmain = jnp.where(clean == 1, inputs, xb)
    edge = jnp.where(half == 0, inputs[:, rows - HALO :], inputs[:, :HALO])
    xc = lax.ppermute(jnp.concatenate([xmain[:, rows - win :], edge], axis=1), "seq", pairs)
    start = half * rows
    edge_at = jnp.where(half == 0, rows, -HALO)
    positions = start + jnp.concatenate([jnp.arange(-win, rows), edge_at + jnp.arange(HALO)])
    turned = positions.astype(F32)[:, None] * freqs
    sine = jnp.sin(turned)
    cos = jnp.cos(turned)
    sin = jnp.where(jnp.arange(128)[None] % HD < HD // 2, -sine, sine)
    code = segment_ids * SEG_STEP + block_ids
    padded = jnp.pad(code, ((0, 0), (win, 0)), constant_values=-1)
    key_codes = lax.dynamic_slice_in_dim(padded, start, win + rows, 1)
    own_code = lax.dynamic_slice_in_dim(code, start, rows, 1)
    own_seg = lax.dynamic_slice_in_dim(segment_ids, start, rows, 1)
    before, after = code[:, rows - HALO : rows], code[:, rows : rows + HALO]
    codes = jnp.concatenate(
        [
            key_codes,
            jnp.where((clean == 1) & (half == 0), after, -1),
            jnp.where((clean == 0) & (half == 1), before, -2),
            jnp.where(clean == 0, own_code, -2),
            jnp.where((clean == 0) & (half == 0), after, -2),
            jnp.full((micro, keys - lay["used"]), -2, jnp.int32),
        ],
        axis=1,
    )[:, :, None].astype(F32)
    queries = jnp.stack([own_seg * SEG_STEP, own_code - (1 - clean), own_code], axis=1)
    queries = jnp.concatenate([queries, jnp.zeros((micro, 5, rows), jnp.int32)], axis=1).astype(F32)
    packed = lax.all_gather(jnp.concatenate(small)[None], "fsdp", axis=0, tiled=True)
    vectors, at = [], 0
    longest = max(sizes) * packed.shape[0]
    for size in sizes:
        one = packed[:, at : at + size].reshape(-1).astype(F32)
        vectors.append(jnp.pad(one, (0, longest - one.shape[0])))
        at += size
    vec = jnp.stack(vectors)
    w_in, w_out, w_up, w_down = (lax.all_gather(p, "fsdp", axis=0, tiled=True) for p in weights)
    per_seq = lambda n, d: pl.BlockSpec((1, n, d), lambda s: (s, 0, 0))
    table_rows = win + rows + HALO
    q, k, v, a = call(
        functools.partial(qkv_kernel, lay), (micro,),
        [SMEM(), per_seq(rows, width), per_seq(rows, width), per_seq(win + HALO, width),
         whole((width, 3 * width)), whole(vec.shape), whole((table_rows, 128)), whole((table_rows, 128))],
        [per_seq(rows, width), per_seq(keys, width), per_seq(keys, width), per_seq(keys, width)],
        [like((micro, rows, width), BF16)] + [like((micro, keys, width), BF16)] * 3,
        [], 2 * micro * rows * width * 3 * width * 2, 20 << 20, "qkv",
    )(role, inputs, xb, xc, w_in, vec, cos, sin)
    qw = QUAD * HD
    quads = width // qw
    quad_block = lambda n: pl.BlockSpec((1, n, qw), lambda s, h: (s, 0, h))
    o, lse = call(
        functools.partial(attend_kernel, lay), (micro, quads),
        [pl.BlockSpec((1, keys, 1), lambda s, h: (s, 0, 0)), pl.BlockSpec((1, 8, rows), lambda s, h: (s, 0, 0)),
         quad_block(rows), quad_block(keys), quad_block(keys)],
        [quad_block(rows), pl.BlockSpec((1,) + lse_shape[1:], lambda s, h: (s * quads + h, 0, 0))],
        [like((micro, rows, width), BF16), like(lse_shape, F32)],
        bias_scratch, 2 * attn_flops, 12 << 20, "attend",
    )(codes, queries, q, k, v)
    return w_in, w_out, w_up, w_down, q, k, v, a, o, lse, vec, cos, sin, codes, queries


def back_remote(
    lay, role, sizes, inputs, cotangent, codes, queries, lse, cos, sin, vec,
    q, k, v, o, a, w_in, w_out, w_up, w_down, bias_scratch, attn_flops,
):
    micro, rows, width = inputs.shape
    keys, win = lay["keys"], lay["win"]
    bits = lax.axis_size("fsdp").bit_length() - 1
    lead = (2,) * bits
    count = 1 << bits
    hidden = w_up.shape[1]
    slab, slab_down = width // count, hidden // count
    third = width // 2
    steps, wide = slab_down // 128, count // 2 * 128

    def bank(name, r, c):
        over_x = BACK_BITS[name][1]
        kept = r // 2 if over_x else r
        over = [pltpu.VMEM(lead[: bits - 1 - b] + (kept, c), BF16) for b in range(bits)]
        ends = [pltpu.VMEM(lead + (kept, c), BF16)] if over_x else []
        return pltpu.VMEM(lead + (r, c), BF16), tuple(ends + over + ([] if over_x else [pltpu.VMEM((r, c), BF16)]))

    acc_in, r_in = zip(*[bank("i%d" % j, slab, third) for j in range(3)])
    acc_out, r_out = bank("o", slab, width // 2)
    acc_up, r_up = zip(*[bank("u%d" % j, slab, wide) for j in range(steps)])
    acc_down, r_down = zip(*[bank("d%d" % j, 128, width // 2) for j in range(steps)])
    stages = 2 + bits
    remote = (7 + 2 * steps) * (bits + 5) + 2 * stages + 4 * micro
    scratch = [
        pltpu.VMEM((micro, rows, width), BF16), pltpu.VMEM((micro, rows, width), BF16),
        pltpu.VMEM((micro, win + HALO, width), BF16),
        acc_in, acc_out, acc_up, acc_down, r_in, r_out, r_up, r_down,
        pltpu.VMEM((slab, 3 * width), BF16), pltpu.VMEM((slab, width), BF16),
        pltpu.VMEM((steps, slab, count * 128), BF16), pltpu.VMEM((slab_down, width), BF16),
        pltpu.VMEM((8, hidden), F32), pltpu.VMEM((2 * stages, 8, hidden), F32),
        pltpu.VMEM((8, width), F32), pltpu.VMEM((2 * stages, 8, width), F32),
        pltpu.SemaphoreType.DMA((remote,)), pltpu.SemaphoreType.DMA((remote,)),
        pltpu.SemaphoreType.DMA((8 + steps * count,)),
    ] + bias_scratch
    out_rows, grad_in, f_in, f_out, f_up, f_down, sums, late = pl.pallas_call(
        functools.partial(back_kernel, lay, bits),
        in_specs=[VMEM] * 8 + [ANY] * 9,
        out_specs=[ANY] * 6 + [VMEM] * 2,
        out_shape=[
            like((micro, rows, width), BF16), like((micro, rows, width), F32), like((slab, 3 * width), BF16),
            like((slab, width), BF16), like((slab, hidden), BF16), like((slab_down, width), BF16),
            like((8, hidden), F32), like((8, width), F32),
        ],
        scratch_shapes=scratch,
        compiler_params=pltpu.CompilerParams(
            vmem_limit_bytes=67043328, collective_id=1, has_side_effects=True
        ),
        cost_estimate=pl.CostEstimate(flops=6 * attn_flops, bytes_accessed=60 << 20, transcendentals=0),
        name="back",
    )(codes, queries, lse, cos, sin, vec, inputs, o, cotangent.reshape(micro * rows, width),
      q, k, v, a, w_in, w_out, w_up, w_down)
    big_shapes = [like(g.shape, F32) for g in (f_in, f_out, f_up, f_down)]
    done = pl.pallas_call(
        functools.partial(finish_kernel, sizes),
        in_specs=[VMEM] * 6,
        out_specs=[VMEM] * 12,
        out_shape=big_shapes + [like((size,), F32) for size in sizes],
        compiler_params=pltpu.CompilerParams(vmem_limit_bytes=VMEM_BYTES),
        cost_estimate=pl.CostEstimate(flops=0, bytes_accessed=6 << 20, transcendentals=0),
        name="finish",
    )(sums, late, f_in, f_out, f_up, f_down)
    return out_rows, grad_in, list(done[:4]), list(done[4:])


def back_native(
    lay, role, sizes, inputs, cotangent, codes, queries, lse, cos, sin, vec,
    q, k, v, o, a, w_in, w_out, w_up, w_down, bias_scratch, attn_flops,
):
    micro, rows, width = inputs.shape
    keys, win = lay["keys"], lay["win"]
    clean, half = role[0], role[1]
    pairs = [(0, 1), (1, 0), (2, 3), (3, 2)]
    fsdp_n = lax.axis_size("fsdp")
    hidden = w_up.shape[1]
    qw = QUAD * HD
    quads = width // qw
    total = micro * rows
    flat = lambda z: z.reshape(total, width)
    chunk = min(512, hidden)
    rows_spec = whole((total, width))
    out_rows, dx2, do, g_w_out, g_w_up, g_b_up, g_w_down, g_mlp = call(
        mlp_kernel, (hidden // chunk,),
        [rows_spec, rows_spec, rows_spec, whole((width, width)), whole(vec.shape),
         pl.BlockSpec((width, chunk), lambda j: (0, j)), pl.BlockSpec((8, chunk), lambda j: (0, j)),
         pl.BlockSpec((chunk, width), lambda j: (j, 0))],
        [rows_spec, rows_spec, rows_spec, whole((width, width)),
         pl.BlockSpec((width, chunk), lambda j: (0, j)), pl.BlockSpec((8, chunk), lambda j: (0, j)),
         pl.BlockSpec((chunk, width), lambda j: (j, 0)), whole((8, width))],
        [like((total, width), BF16), like((total, width), F32), like((total, width), BF16),
         like((width, width), BF16), like((width, hidden), BF16), like((8, hidden), F32),
         like((hidden, width), BF16), like((8, width), F32)],
        [pltpu.VMEM((total, width), F32), pltpu.VMEM((total, width), BF16), pltpu.VMEM((width, total), BF16),
         pltpu.VMEM((total, 1), F32), pltpu.VMEM((total, width), F32), pltpu.VMEM((total, width), F32)],
        2 * total * width * (6 * hidden + 3 * width), 40 << 20, "mlp",
    )(flat(o), flat(inputs), flat(cotangent), w_out, vec, w_up, vec, w_down)

    do = do.reshape(micro, rows, width)
    per_seq = lambda n, d: pl.BlockSpec((1, n, d), lambda s: (s, 0, 0))
    role_spec = SMEM()
    quad_block = lambda n: pl.BlockSpec((1, n, qw), lambda s, h: (s, 0, h))
    code_spec = pl.BlockSpec((1, keys, 1), lambda s, h: (s, 0, 0))
    query_spec = pl.BlockSpec((1, 8, rows), lambda s, h: (s, 0, 0))
    lse_spec = pl.BlockSpec((1,) + lse.shape[1:], lambda s, h: (s * quads + h, 0, 0))
    table = pl.BlockSpec((win + rows + HALO, 128), lambda s, h: (0, 0), pipeline_mode=pl.Buffered(1))
    dq, dk, dv = call(
        functools.partial(attend_back_kernel, lay), (micro, quads),
        [code_spec, query_spec, quad_block(rows), quad_block(keys), quad_block(keys),
         quad_block(rows), quad_block(rows), lse_spec, table, table],
        [quad_block(rows), quad_block(keys), quad_block(keys)],
        [like((micro, rows, width), BF16), like((micro, keys, width), BF16), like((micro, keys, width), BF16)],
        [pltpu.VMEM((keys, qw), F32), pltpu.VMEM((keys, qw), F32)] + bias_scratch,
        5 * attn_flops, 24 << 20, "attend_back",
    )(codes, queries, q, k, v, o, do, lse, cos, sin)

    da_own, da_main, da_win, g_w_in, g_b_in = call(
        functools.partial(qkv_back_kernel, lay), (micro,),
        [role_spec, per_seq(keys, width), per_seq(rows, width), per_seq(keys, width), per_seq(keys, width),
         whole((width, 3 * width))],
        [per_seq(rows, width), per_seq(rows, width), per_seq(win + HALO, width),
         whole((width, 3 * width)), whole((8, 3 * width))],
        [like((micro, rows, width), F32), like((micro, rows, width), BF16), like((micro, win + HALO, width), BF16),
         like((width, 3 * width), BF16), like((8, 3 * width), F32)],
        [pltpu.VMEM((width, 3 * width), F32)], 2 * 2 * micro * rows * width * 3 * width * 2, 40 << 20, "qkv_back",
    )(role, a, dq, dk, dv, w_in)

    from_pair = lax.ppermute(da_win, "seq", pairs).astype(F32)
    from_second = jnp.where(half == 0, from_pair[:, :win], 0.0)
    edge = from_pair[:, win:]
    gap = jnp.zeros((micro, rows - HALO, width), F32)
    edges = jnp.where(
        half == 0, jnp.concatenate([gap, edge], axis=1), jnp.concatenate([edge, gap], axis=1)
    )
    added = jnp.pad(from_second, ((0, 0), (rows - win, 0), (0, 0)))
    to_clean = (jnp.where(clean == 0, da_main.astype(F32), 0.0) + added).astype(BF16)
    from_noisy = lax.ppermute(to_clean, "seq", [(0, 2), (1, 3)])
    extra = jnp.where(clean == 1, from_noisy.astype(F32) + added, 0.0) + edges

    grad_in, g_attn = call(
        final_kernel, (2,),
        [pl.BlockSpec((total // 2, width), lambda i: (i, 0))] * 4 + [whole((1, width))],
        [pl.BlockSpec((total // 2, width), lambda i: (i, 0)), whole((8, width))],
        [like((total, width), F32), like((8, width), F32)], [], 0, 16 << 20, "norm_back",
    )(flat(inputs), flat(da_own), flat(extra), flat(dx2), vec[0:1, :width])

    def scatter(g):
        return lax.psum(lax.psum_scatter(g, "fsdp", scatter_dimension=0, tiled=True), "seq")

    big = [scatter(g).astype(F32) for g in (g_w_in, g_w_out, g_w_up, g_w_down)]
    smalls = [g_attn[0], g_attn[1], g_b_in[0], g_mlp[3], g_mlp[1], g_mlp[2], g_b_up[0], g_mlp[0]]
    pack = jnp.concatenate([g.reshape(fsdp_n, -1) for g in smalls], axis=1)
    pack = lax.psum(pack, ("seq", "fsdp"))
    mine = lax.dynamic_slice_in_dim(pack, lax.axis_index("fsdp"), 1, 0)[0]
    outs, at = [], 0
    for size in sizes:
        outs.append(mine[at : at + size])
        at += size
    return out_rows.reshape(micro, rows, width), grad_in.reshape(micro, rows, width), big, outs


def per_device(
    inputs, segment_ids, block_ids, attn_gain, attn_shift, proj_in, bias_in, proj_out, bias_out,
    mlp_gain, mlp_shift, weight_up, bias_up, weight_down, bias_down, cotangent,
):
    micro, rows, width = inputs.shape
    length = segment_ids.shape[1]
    hidden = weight_up.shape[1]
    seq_n = lax.axis_size("seq")
    fsdp_n = lax.axis_size("fsdp")
    assert seq_n == 4 and seq_n * rows == 2 * length
    lay = layout(rows, length)
    win, keys = lay["win"], lay["keys"]
    me = lax.axis_index("seq")
    clean = me // 2
    half = me % 2
    role = jnp.stack([clean, half]).astype(jnp.int32)
    pairs = [(0, 1), (1, 0), (2, 3), (3, 2)]
    small = (attn_gain, attn_shift, bias_in, bias_out, mlp_gain, mlp_shift, bias_up, bias_down)
    sizes = [p.shape[0] for p in small]
    weights = (proj_in, proj_out, weight_up, weight_down)
    half_dim = HD // 2
    freqs = (10000.0 ** (-(np.arange(half_dim, dtype=np.float32) / half_dim))).astype(np.float32)
    freqs = np.tile(freqs, 4)[None]
    quads = width // (QUAD * HD)
    qw = QUAD * HD
    spans = [hi - lo + NEAR for lo, hi in windows(lay)]
    bias_scratch = [pltpu.VMEM((rows // TILE, max(spans), TILE), F32)]
    per_seq = lambda n, d: pl.BlockSpec((1, n, d), lambda s: (s, 0, 0))
    role_spec = SMEM()
    attn_flops = micro * quads * sum(spans) * QUAD * TILE * qw * 2
    lse_shape = (micro * quads, rows // TILE, QUAD * TILE)
    table_rows = win + rows + HALO
    aligned = fsdp_n & (fsdp_n - 1) == 0 and all(p.shape[0] % (4 * HALO) in (0, 32) for p in weights)
    front = front_remote if aligned else front_native
    (w_in, w_out, w_up, w_down, q, k, v, a, o, lse, vec, cos, sin, codes, queries) = front(
        lay, role, sizes, inputs, segment_ids, block_ids, small, weights, freqs,
        lse_shape, bias_scratch, spans, attn_flops,
    )
    back = back_remote if aligned else back_native
    out_rows, grad_in, big, vectors = back(
        lay, role, sizes, inputs, cotangent, codes, queries, lse, cos, sin, vec,
        q, k, v, o, a, w_in, w_out, w_up, w_down, bias_scratch, attn_flops,
    )
    g_gain1, g_shift1, g_bin, g_bout, g_gain2, g_shift2, g_bup, g_bdown = vectors
    return (
        out_rows, grad_in, g_gain1, g_shift1, big[0], g_bin, big[1], g_bout,
        g_gain2, g_shift2, big[2], g_bup, big[3], g_bdown,
    )


def solution(mesh):
    rows = P("fsdp", "seq", None)
    one, two = P("fsdp"), P("fsdp", None)
    params = (one, one, two, one, two, one, one, one, two, one, two, one)
    return jax.shard_map(
        per_device,
        mesh=mesh,
        in_specs=(rows, two, two) + params + (rows,),
        out_specs=(rows, rows) + params,
        check_vma=False,
    )
```

profile of v0, /device:TPU:0, one launch (start us, length us, event | category | flops | bytes accessed | tf_op | source)
XLA Modules:
  0.0 255.3 jit_solution(11281449819723343174)
XLA Ops:
  0.7 91.6 %front.1 = (bf16[2,2,2,96,2304]{4,3,2,1,0:T(8,128)(2,1)}, bf16[2,2,2,96,768]{4,3,2,1,0:T(8,128)(2,1)}, bf16[2,2,2,96,3072]{4,3,2,1,0:T(8,128)(2,1)}, bf16[2,2,2,...) custom-call(bf16[2,512,768]{2,1,0:T(8,128)(2,1)} %x.3, ...), custom_call_target="tpu_custom_call" | custom-call | flops 9462349824 | bytes 41943040 | tf_op jit(solution)/shard_map/front/pallas_call | solution.py:1562
  92.3 155.3 %back.1 = (bf16[2,512,768]{2,1,0:T(8,128)(2,1)}, f32[2,512,768]{2,1,0:T(8,128)}, bf16[96,2304]{1,0:T(8,128)(2,1)}, bf16[96,768]{1,0:T(8,128)(2,1)}, bf16[96,3072...) custom-call(f32[2,1536,1]{2,1,0:T(8,128)} %get-tuple-element.49.codes, ...), custom_call_target="tpu_custom_call" | custom-call | flops 28387049472 | bytes 62914560 | tf_op jit(solution)/shard_map/back/pallas_call | solution.py:1694
  247.6 0.0 copy-start.1
  247.6 3.5 %finish.1 = (f32[96,2304]{1,0:T(8,128)}, f32[96,768]{1,0:T(8,128)}, f32[96,3072]{1,0:T(8,128)}, f32[384,768]{1,0:T(8,128)}, f32[96]{0:T(128)}, /*index=5*/f32[96...) custom-call(f32[8,3072]{1,0:T(8,128)} %get-tuple-element.66.sums, ...), custom_call_target="tpu_custom_call" | custom-call | bytes 6291456 | tf_op jit(solution)/shard_map/finish/pallas_call | solution.py:1712
  251.2 0.0 copy-done.1
  251.2 0.0 copy-start
  251.2 1.1 copy.33
  252.3 1.3 copy-done
  253.6 1.7 copy.34
Async XLA Ops:
  247.6 3.6 %copy-start.1 = (bf16[2,512,768]{2,1,0:T(8,128)(2,1)S(1)}, bf16[2,512,768]{2,1,0:T(8,128)(2,1)}, u32[]{:S(2)}) copy-start(bf16[2,512,768]{2,1,0:T(8,128)(2,1)} %get-tuple-element.98) | copy-start | bytes 4718596
  251.2 2.5 copy-start
where the time goes:
time: 256 us; the launch traced here: 255 us
  Pallas kernels  250 us (98%)
  local copies, waits for them, and re-layouts  4.12 us (2%)
    pallas_call x1, Pallas kernels, back_remote(): pl.pallas_call(functools.partial(back_kernel, lay, bits), in_specs=[VMEM]...  155 us
    pallas_call x1, Pallas kernels, front_remote(): pl.pallas_call(functools.partial(front_kernel, lay, bits, sizes), in_spec...  91.6 us

commit v1 on v0

--- a/solution.py
+++ b/solution.py
@@ -403,22 +403,22 @@
 
 FRONT_ORDER = (
     "E s i0 i1",
-    "T s R0 i2",
+    "T s i2 R0",
     "i0 i1 i2 i0",
-    "u0 s i1 s",
-    "u1 i2 o i1",
-    "V u0 i0 R1",
-    "u1 i1 i2 i0",
-    "o d0 P0 L0",
-    "L1 W H i2",
-    "u0 L2 u1 O0",
-    "O1 O2 d1 u0",
-    "o d0 A d1",
-    "P1 d0 u1 A",
-    "A d1 o u0",
-    "A u0 d0 u1",
-    "A d1 d0 A",
-    "o u1",
+    "u0 s i1 u1",
+    "i2 s o i1",
+    "i1 V u0 i0",
+    "R1 u1 i2 o",
+    "i0 d0 L0 W",
+    "P0 i2 L2 u0",
+    "L1 H u1 d1",
+    "O0 O1 O2 u0",
+    "o d0 d1 A",
+    "P1 u1 A d0",
+    "A d1 u0 A",
+    "u0 d0 u1 o",
+    "A d1 A o",
+    "u1 d0",
 )
 FRONT_BITS = {
     "i0": ((2, 0, 1), False),
@@ -1524,9 +1524,22 @@
     )
 
 
-def finish_kernel(sizes, sums, late, g_in, g_out, g_up, g_down, o_in, o_out, o_up, o_down, *vectors):
-    for src, dst in ((g_in, o_in), (g_out, o_out), (g_up, o_up), (g_down, o_down)):
-        dst[...] = src[...].astype(F32)
+def finish_kernel(sizes, sums, late, *refs):
+    given, results, vectors, rest = refs[:6], refs[6:12], refs[12:20], refs[20:]
+    held, wide, sem_in, sem_out = rest[:6], rest[6:10], rest[10], rest[11]
+    loads = [pltpu.make_async_copy(src, dst, sem_in.at[n]) for n, (src, dst) in enumerate(zip(given, held))]
+    stores = [
+        pltpu.make_async_copy(src, dst, sem_out.at[n]) for n, (src, dst) in enumerate(zip(held[:2] + wide, results))
+    ]
+    for load in loads:
+        load.start()
+    for n in range(2):
+        loads[n].wait()
+        stores[n].start()
+    for n in range(4):
+        loads[2 + n].wait()
+        wide[n][...] = held[2 + n][...].astype(F32)
+        stores[2 + n].start()
     f = lax.axis_index("fsdp")
     width = late.shape[1]
     for r, (size, out) in enumerate(zip(sizes, vectors)):
@@ -1540,6 +1553,8 @@
         row = jnp.broadcast_to(row, (8, whole_size))
         turned = pltpu.roll(row, lax.rem(whole_size - f * size, whole_size), 1)
         out[...] = turned[0, :size]
+    for store in stores:
+        store.wait()
 
 
 def front_remote(
@@ -1708,17 +1723,21 @@
         name="back",
     )(codes, queries, lse, cos, sin, vec, inputs, o, cotangent.reshape(micro * rows, width),
       q, k, v, a, w_in, w_out, w_up, w_down)
-    big_shapes = [like(g.shape, F32) for g in (f_in, f_out, f_up, f_down)]
+    shards = (f_in, f_out, f_up, f_down)
+    given = (out_rows, grad_in) + shards
     done = pl.pallas_call(
         functools.partial(finish_kernel, sizes),
-        in_specs=[VMEM] * 6,
-        out_specs=[VMEM] * 12,
-        out_shape=big_shapes + [like((size,), F32) for size in sizes],
+        in_specs=[VMEM] * 2 + [ANY] * 6,
+        out_specs=[ANY] * 6 + [VMEM] * 8,
+        out_shape=[like(out_rows.shape, BF16), like(grad_in.shape, F32)]
+        + [like(g.shape, F32) for g in shards] + [like((size,), F32) for size in sizes],
+        scratch_shapes=[pltpu.VMEM(g.shape, g.dtype) for g in given] + [pltpu.VMEM(g.shape, F32) for g in shards]
+        + [pltpu.SemaphoreType.DMA((6,)), pltpu.SemaphoreType.DMA((6,))],
         compiler_params=pltpu.CompilerParams(vmem_limit_bytes=VMEM_BYTES),
-        cost_estimate=pl.CostEstimate(flops=0, bytes_accessed=6 << 20, transcendentals=0),
+        cost_estimate=pl.CostEstimate(flops=0, bytes_accessed=16 << 20, transcendentals=0),
         name="finish",
-    )(sums, late, f_in, f_out, f_up, f_down)
-    return out_rows, grad_in, list(done[:4]), list(done[4:])
+    )(sums, late, *given)
+    return done[0], done[1], list(done[2:6]), list(done[6:])
 
 
 def back_native(

time: 256 us -> 254 us (level)
  local copies, waits for them, and re-layouts: 4.12 us -> 0 us
  Pallas kernels: 250 us -> 253 us
    unnamed x6 -> x0, local copies, waits for them, and re-layouts: 4.12 us -> none
    pallas_call x1, Pallas kernels: 3.54 us -> 6.72 us  [back_remote(): pl.pallas_call(functools.partial(finish_kernel, sizes), in_specs=[VMEM] *...]
where the time goes in v1:
time: 254 us
  Pallas kernels  253 us (100%)
    pallas_call x1, Pallas kernels, back_remote(): pl.pallas_call(functools.partial(back_kernel, lay, bits), in_specs=[VMEM]...  154 us
    pallas_call x1, Pallas kernels, front_remote(): pl.pallas_call(functools.partial(front_kernel, lay, bits, sizes), in_spec...  91.9 us
    pallas_call x1, Pallas kernels, back_remote(): pl.pallas_call(functools.partial(finish_kernel, sizes), in_specs=[VMEM] *...  6.72 us

profile of v1, /device:TPU:0, one launch (start us, length us, event | category | flops | bytes accessed | tf_op | source)
XLA Modules:
  0.0 253.8 jit_solution(14565494459349417761)
XLA Ops:
  0.7 91.9 %front.1 = (bf16[2,2,2,96,2304]{4,3,2,1,0:T(8,128)(2,1)}, bf16[2,2,2,96,768]{4,3,2,1,0:T(8,128)(2,1)}, bf16[2,2,2,96,3072]{4,3,2,1,0:T(8,128)(2,1)}, bf16[2,2,2,...) custom-call(bf16[2,512,768]{2,1,0:T(8,128)(2,1)} %x.3, ...), custom_call_target="tpu_custom_call" | custom-call | flops 9462349824 | bytes 41943040 | tf_op jit(solution)/shard_map/front/pallas_call | solution.py:1577
  92.6 154.3 %back.1 = (bf16[2,512,768]{2,1,0:T(8,128)(2,1)}, f32[2,512,768]{2,1,0:T(8,128)}, bf16[96,2304]{1,0:T(8,128)(2,1)}, bf16[96,768]{1,0:T(8,128)(2,1)}, bf16[96,3072...) custom-call(f32[2,1536,1]{2,1,0:T(8,128)} %get-tuple-element.51.codes, ...), custom_call_target="tpu_custom_call" | custom-call | flops 28387049472 | bytes 62914560 | tf_op jit(solution)/shard_map/back/pallas_call | solution.py:1709
  246.9 6.7 %finish.1 = (bf16[2,512,768]{2,1,0:T(8,128)(2,1)}, f32[2,512,768]{2,1,0:T(8,128)}, f32[96,2304]{1,0:T(8,128)}, f32[96,768]{1,0:T(8,128)}, f32[96,3072]{1,0:T(8,1...) custom-call(f32[8,3072]{1,0:T(8,128)} %get-tuple-element.66.sums, ...), custom_call_target="tpu_custom_call" | custom-call | bytes 16777216 | tf_op jit(solution)/shard_map/finish/pallas_call | solution.py:1728

commit v2 on v1

--- a/solution.py
+++ b/solution.py
@@ -472,7 +472,7 @@
     lay, bits, sizes, x, seg, blk, freqs, w_in_s, w_out_s, w_up_s, w_down_s,
     small0, small1, small2, small3, small4, small5, small6, small7,
     w_in, w_out, w_up, w_down, q_out, k_out, v_out, a_out, o_out, lse_out, vec, cos, sin, codes, queries,
-    xb, xc, w_vm, q, k, v, a, o, lse, packs, pack, send, recv, sems, *biases,
+    xb, xc, w_vm, q, k, v, a, o, lse, packs, pack, coarse, send, recv, sems, *biases,
 ):
     rows, win, length = lay["rows"], lay["win"], lay["length"]
     width = x.shape[2]
@@ -535,23 +535,25 @@
     count = 1 << bits
 
     def tables():
-        block = 48
-        assert (win + rows + HALO) % block == 0
+        blocks = (win + rows) // HALO
+        number = lax.broadcasted_iota(jnp.int32, (-(-(blocks + 1) // 8) * 8, 128), 0)
+        begin = jnp.where(number < blocks, number * HALO - win, jnp.where(second, -HALO, rows))
+        turned = (begin + jnp.where(second, rows, 0)).astype(F32) * freqs[...]
+        coarse[0] = jnp.cos(turned)
+        coarse[1] = jnp.sin(turned)
+        inside = lax.broadcasted_iota(jnp.int32, (HALO, 128), 0).astype(F32) * freqs[...]
+        fine_cos, fine_sin = jnp.cos(inside), jnp.sin(inside)
+        lane = lax.broadcasted_iota(jnp.int32, (HALO, 128), 1)
+        sign = jnp.where(lane % HD < HD // 2, -1.0, 1.0)
 
         def table_step(n, carry):
-            span = pl.ds(pl.multiple_of(n * block, HALO), block)
-            position = lax.broadcasted_iota(jnp.int32, (block, 128), 0) + n * block
-            shifted = jnp.where(
-                position < win + rows, position - win, position - win - rows + jnp.where(second, -HALO, rows)
-            )
-            turned = (shifted + jnp.where(second, rows, 0)).astype(F32) * freqs[...]
-            lane = lax.broadcasted_iota(jnp.int32, (block, 128), 1)
-            cos[span, :] = jnp.cos(turned)
-            sine = jnp.sin(turned)
-            sin[span, :] = jnp.where(lane % HD < HD // 2, -sine, sine)
+            span = pl.ds(pl.multiple_of(n * HALO, HALO), HALO)
+            c, sn = coarse[0, pl.ds(n, 1), :], coarse[1, pl.ds(n, 1), :]
+            cos[span, :] = c * fine_cos - sn * fine_sin
+            sin[span, :] = (sn * fine_cos + c * fine_sin) * sign
             return carry
 
-        lax.fori_loop(0, (win + rows + HALO) // block, table_step, 0)
+        lax.fori_loop(0, blocks + 1, table_step, 0)
         code = (seg[...] * SEG_STEP + blk[...]).astype(F32)
         base = (seg[...] * SEG_STEP).astype(F32)
         turned_code = jnp.transpose(jnp.concatenate([code, jnp.zeros((8 - micro, length), F32)], axis=0))
@@ -1585,6 +1587,7 @@
             pltpu.VMEM((micro, keys, width), BF16), pltpu.VMEM((micro, keys, width), BF16),
             pltpu.VMEM((micro, keys, width), BF16), pltpu.VMEM((micro, rows, width), BF16),
             pltpu.VMEM(lse_shape, F32), pltpu.VMEM((2,) * bits + (8, lanes), F32), pltpu.VMEM((8, lanes), F32),
+            pltpu.VMEM((2, -(-(table_rows // HALO) // 8) * 8, 128), F32),
             pltpu.SemaphoreType.DMA((remote,)), pltpu.SemaphoreType.DMA((remote,)),
             pltpu.SemaphoreType.DMA((96,)),
         ] + bias_scratch,

time: 254 us -> 254 us (level)
  no operation moved by 1% of the time
where the time goes in v2:
time: 254 us
  Pallas kernels  253 us (100%)
    pallas_call x1, Pallas kernels, back_remote(): pl.pallas_call(functools.partial(back_kernel, lay, bits), in_specs=[VMEM]...  154 us
    pallas_call x1, Pallas kernels, front_remote(): pl.pallas_call(functools.partial(front_kernel, lay, bits, sizes), in_spec...  92 us
    pallas_call x1, Pallas kernels, back_remote(): pl.pallas_call(functools.partial(finish_kernel, sizes), in_specs=[VMEM] *...  6.72 us

profile of v2, /device:TPU:0, one launch (start us, length us, event | category | flops | bytes accessed | tf_op | source)
XLA Modules:
  0.0 253.7 jit_solution(13603506707087628041)
XLA Ops:
  0.7 92.0 %front.1 = (bf16[2,2,2,96,2304]{4,3,2,1,0:T(8,128)(2,1)}, bf16[2,2,2,96,768]{4,3,2,1,0:T(8,128)(2,1)}, bf16[2,2,2,96,3072]{4,3,2,1,0:T(8,128)(2,1)}, bf16[2,2,2,...) custom-call(bf16[2,512,768]{2,1,0:T(8,128)(2,1)} %x.3, ...), custom_call_target="tpu_custom_call" | custom-call | flops 9462349824 | bytes 41943040 | tf_op jit(solution)/shard_map/front/pallas_call | solution.py:1579
  92.6 154.2 %back.1 = (bf16[2,512,768]{2,1,0:T(8,128)(2,1)}, f32[2,512,768]{2,1,0:T(8,128)}, bf16[96,2304]{1,0:T(8,128)(2,1)}, bf16[96,768]{1,0:T(8,128)(2,1)}, bf16[96,3072...) custom-call(f32[2,1536,1]{2,1,0:T(8,128)} %get-tuple-element.51.codes, ...), custom_call_target="tpu_custom_call" | custom-call | flops 28387049472 | bytes 62914560 | tf_op jit(solution)/shard_map/back/pallas_call | solution.py:1712
  246.8 6.7 %finish.1 = (bf16[2,512,768]{2,1,0:T(8,128)(2,1)}, f32[2,512,768]{2,1,0:T(8,128)}, f32[96,2304]{1,0:T(8,128)}, f32[96,768]{1,0:T(8,128)}, f32[96,3072]{1,0:T(8,1...) custom-call(f32[8,3072]{1,0:T(8,128)} %get-tuple-element.66.sums, ...), custom_call_target="tpu_custom_call" | custom-call | bytes 16777216 | tf_op jit(solution)/shard_map/finish/pallas_call | solution.py:1731
